TPU v7x, 256 devices: a whole 4x4x8 slice. The times are simulated.
256 devices in a mesh: dp: 16 (over x, y), tensor: 16 (over z, core).
Axes of the slice: x: 4, y: 4, z: 8, core: 2. Of those that a mesh axis runs over, the one named last changes fastest.
Arguments:
- tokens: bfloat16 [1024, 8192], P('tensor', 'dp'), may hold values from -6 to 6
- grad_output: bfloat16 [1024, 8192], P('tensor', 'dp'), may hold values from -6 to 6
- gate_weight: bfloat16 [8192, 14336], P('dp', 'tensor'), may hold values from -0.09375 to 0.09375
- up_weight: bfloat16 [8192, 14336], P('dp', 'tensor'), may hold values from -0.09375 to 0.09375
- down_weight: bfloat16 [14336, 8192], P('tensor', 'dp'), may hold values from -0.0625 to 0.0625
- gate_mask: int32 [64, 112], P('dp', 'tensor'), may hold values 0 or 1
- up_mask: int32 [64, 112], P('dp', 'tensor'), may hold values 0 or 1
- down_mask: int32 [112, 64], P('tensor', 'dp'), may hold values 0 or 1
Outputs:
- output: bfloat16 [1024, 8192], P('tensor', 'dp')
- grad_tokens: bfloat16 [1024, 8192], P('tensor', 'dp')
- grad_gate: bfloat16 [8192, 14336], P('dp', 'tensor')
- grad_up: bfloat16 [8192, 14336], P('dp', 'tensor')
- grad_down: bfloat16 [14336, 8192], P('tensor', 'dp')
All inputs are finite; a program needn't handle non-finite values. No bound on the sum of `gate_mask` or of `up_mask` or of `down_mask` on one device may be relied on, other than what follows from the above.
Results may differ from a plain program's by a relative error of at most 0.005.
Values may be sent and summed in bfloat16 or wider, within the bound.
A program may use at most 128 MiB of HBM per device.

v0:
```python
import jax
import jax.numpy as jnp
from jax import lax
from jax.sharding import PartitionSpec as P


def spread(mask_table, weight):
    side = weight.shape[0] // mask_table.shape[0]
    return jnp.repeat(jnp.repeat(mask_table, side, axis=0), side, axis=1).astype(jnp.bfloat16)


def contract_rows(left, right_side):
    return lax.dot_general(
        left, right_side, (((0,), (0,)), ((), ())), preferred_element_type=jnp.float32
    )


def contract_cols(left, right_side):
    return lax.dot_general(
        left, right_side, (((1,), (1,)), ((), ())), preferred_element_type=jnp.float32
    )


def shards(tokens, grad_output, gate_weight, up_weight, down_weight, gate_mask, up_mask, down_mask):
    gate_keep = spread(gate_mask, gate_weight)
    up_keep = spread(up_mask, up_weight)
    down_keep = spread(down_mask, down_weight)
    gate_eff = gate_weight * gate_keep
    up_eff = up_weight * up_keep
    down_eff = down_weight * down_keep
    rows_all, cotangents = (
        lax.all_gather(tokens, "tensor", axis=0, tiled=True),
        lax.all_gather(grad_output, "tensor", axis=0, tiled=True),
    )
    part_gate = jnp.dot(rows_all, gate_eff, preferred_element_type=jnp.float32)
    part_up = jnp.dot(rows_all, up_eff, preferred_element_type=jnp.float32)
    share_rows = rows_all.shape[0] // lax.axis_size("dp")
    gate_full, up_full = lax.psum((part_gate, part_up), "dp")
    hidden_all = (gate_full * jax.nn.sigmoid(gate_full) * up_full).astype(jnp.bfloat16)
    first_row = lax.axis_index("dp") * share_rows
    gate_own = lax.dynamic_slice_in_dim(gate_full, first_row, share_rows, 0)
    up_own = lax.dynamic_slice_in_dim(up_full, first_row, share_rows, 0)
    output = lax.psum_scatter(
        jnp.dot(hidden_all, down_eff, preferred_element_type=jnp.float32),
        "tensor",
        scatter_dimension=0,
        tiled=True,
    ).astype(jnp.bfloat16)
    grad_down = (down_keep.astype(jnp.float32) * contract_rows(hidden_all, cotangents)).astype(
        jnp.bfloat16
    )
    part_hidden = contract_cols(cotangents, down_eff)
    grad_hidden = lax.psum_scatter(part_hidden, "dp", scatter_dimension=0, tiled=True)
    sigmoid_gate = jax.nn.sigmoid(gate_own)
    activated = gate_own * sigmoid_gate
    grad_gate_act = (
        grad_hidden * up_own * sigmoid_gate * (1.0 + gate_own * (1.0 - sigmoid_gate))
    ).astype(jnp.bfloat16)
    grad_up_act = (grad_hidden * activated).astype(jnp.bfloat16)
    gate_grads_all, up_grads_all = (
        lax.all_gather(grad_gate_act, "dp", axis=0, tiled=True),
        lax.all_gather(grad_up_act, "dp", axis=0, tiled=True),
    )
    grad_gate = (gate_keep.astype(jnp.float32) * contract_rows(rows_all, gate_grads_all)).astype(
        jnp.bfloat16
    )
    grad_up = (up_keep.astype(jnp.float32) * contract_rows(rows_all, up_grads_all)).astype(
        jnp.bfloat16
    )
    grad_tokens = lax.psum_scatter(
        contract_cols(gate_grads_all, gate_eff) + contract_cols(up_grads_all, up_eff),
        "tensor",
        scatter_dimension=0,
        tiled=True,
    ).astype(jnp.bfloat16)
    return (output, grad_tokens, grad_gate, grad_up, grad_down)


def solution(mesh):
    return jax.shard_map(
        shards,
        mesh=mesh,
        in_specs=(
            P("tensor", "dp"),
            P("tensor", "dp"),
            P("dp", "tensor"),
            P("dp", "tensor"),
            P("tensor", "dp"),
            P("dp", "tensor"),
            P("dp", "tensor"),
            P("tensor", "dp"),
        ),
        out_specs=(
            P("tensor", "dp"),
            P("tensor", "dp"),
            P("dp", "tensor"),
            P("dp", "tensor"),
            P("tensor", "dp"),
        ),
        check_vma=False,
    )
```

profile of v0, /device:TPU:8, one launch (start us, length us, event | category | flops | bytes accessed | tf_op | source)
XLA Modules:
  0.0 554.2 jit_solution(4922906366583342277)
XLA Ops:
  7.2 0.0 copy-start.8
  7.2 0.0 copy-start.7
  7.2 0.0 all-gather.5.cloned.1.call-start
  7.2 0.7 all-gather.5.cloned.1.call-update
  7.9 0.0 all-gather.7.cloned.1.call-start
  8.0 0.7 all-gather.7.cloned.1.call-update
  8.7 0.0 all-reduce.3.cloned.1.call-start
  8.7 0.7 convert_element_type.69
  9.4 0.1 copy.32
  9.5 0.1 broadcast_bitcast_fusion
  9.6 1.5 copy.33
  11.1 0.0 copy-done.8
  11.1 0.1 copy.29
  11.2 0.1 broadcast_bitcast_fusion.1
  11.3 0.0 copy-done.7
  11.3 0.5 copy.30
  11.8 0.1 bitcast_multiply_fusion.2
  11.9 0.1 bitcast_multiply_fusion.3
  12.0 39.4 %all-gather.5.cloned.1.call-done = bf16[1024,512]{1,0:T(8,128)(2,1)} async-done(((bf16[64,512]{1,0:T(8,128)(2,1)}), bf16[1024,512]{1,0:T(8,128)(2,1)}) %all-gather.5.cloned.1.call-update) | async-done | bytes 1048592 | tf_op jit(solution)/shard_map/all_gather | solution.py:32
  51.3 4.5 convolution_bitcast_fusion.1
  55.9 3.2 convolution_bitcast_fusion.2
  59.1 0.0 all-reduce.3.cloned.1.call-update
  59.1 0.0 reduce-scatter.10.cloned.1.call-start
  59.1 0.6 copy-done.9
  59.7 0.1 copy.35
  59.8 30.6 %all-gather.7.cloned.1.call-done = bf16[1024,512]{1,0:T(8,128)(2,1)} async-done(((bf16[64,512]{1,0:T(8,128)(2,1)}), bf16[1024,512]{1,0:T(8,128)(2,1)}) %all-gather.7.cloned.1.call-update) | async-done | bytes 1048592 | tf_op jit(solution)/shard_map/all_gather | solution.py:33
  90.5 1.1 broadcast_in_dim.23
  91.6 0.0 copy-start.1
  91.6 0.9 copy-done.1
  92.5 4.2 convolution_bitcast_fusion
  96.8 5.1 copy.42
  101.8 0.0 reduce-scatter.10.cloned.1.call-update
  101.8 0.0 all-gather.9.cloned.1.call-start
  101.9 132.3 %all-reduce.3.cloned.1.call-done = (f32[1024,896]{1,0:T(8,128)}, f32[1024,896]{1,0:T(8,128)}) async-done(((f32[1024,896]{1,0:T(8,128)}, f32[1024,896]{1,0:T(8,128)}), (f32[1024,896]{1,0:T(8,128)}, f32[1024,896]{1,0:T(8,128)})) %all-reduce.3.cloned.1.call-update) | async-done | bytes 7340048 | tf_op jit(solution)/shard_map/psum | solution.py:38
  234.2 85.4 %reduce-scatter.10.cloned.1.call-done = f32[64,896]{1,0:T(8,128)} async-done(((f32[1024,896]{1,0:T(8,128)}), f32[64,896]{1,0:T(8,128)}) %reduce-scatter.10.cloned.1.call-update) | async-done | bytes 229392 | tf_op jit(solution)/shard_map/reduce_scatter | solution.py:53
  319.5 2.0 multiply_convert_fusion.2
  321.5 0.0 all-gather.9.cloned.1.call-update
  321.5 0.0 all-gather.11.cloned.1.call-start
  321.6 0.5 all-gather.11.cloned.1.call-update
  322.1 0.0 reduce-scatter.6.cloned.1.call-start
  322.1 0.0 copy-start.2
  322.2 0.0 copy-start.6
  322.2 4.3 multiply_convert_fusion
  326.4 1.2 copy-done.4
  327.7 2.6 fusion.2
  330.3 0.0 reduce-scatter.6.cloned.1.call-update
  330.3 0.0 reduce-scatter.8.cloned.1.call-start
  330.4 41.2 %all-gather.9.cloned.1.call-done = bf16[1024,896]{1,0:T(8,128)(2,1)} async-done(((bf16[64,896]{1,0:T(8,128)(2,1)}), bf16[1024,896]{1,0:T(8,128)(2,1)}) %all-gather.9.cloned.1.call-update) | async-done | bytes 1835024 | tf_op jit(solution)/shard_map/all_gather | solution.py:61
  371.5 4.0 fusion.3
  375.6 48.0 %all-gather.11.cloned.1.call-done = bf16[1024,896]{1,0:T(8,128)(2,1)} async-done(((bf16[64,896]{1,0:T(8,128)(2,1)}), bf16[1024,896]{1,0:T(8,128)(2,1)}) %all-gather.11.cloned.1.call-update) | async-done | bytes 1835024 | tf_op jit(solution)/shard_map/all_gather | solution.py:62
  423.6 4.7 convolution_add_fusion
  428.2 0.0 reduce-scatter.8.cloned.1.call-update
  428.3 1.2 copy-done.3
  429.4 4.0 multiply_convert_fusion.1
  433.4 0.1 broadcast_in_dim.19
  433.5 1.2 fusion.1
  434.6 1.3 copy.38
  435.9 0.1 broadcast_in_dim.21
  436.0 2.7 fusion
  438.7 1.3 copy.39
  439.9 45.4 %reduce-scatter.6.cloned.1.call-done = f32[64,512]{1,0:T(8,128)} async-done(((f32[1024,512]{1,0:T(8,128)}), f32[64,512]{1,0:T(8,128)}) %reduce-scatter.6.cloned.1.call-update) | async-done | bytes 131088 | tf_op jit(solution)/shard_map/reduce_scatter | solution.py:43
  485.3 1.5 convert_element_type.76
  486.9 59.0 %reduce-scatter.8.cloned.1.call-done = f32[64,512]{1,0:T(8,128)} async-done(((f32[1024,512]{1,0:T(8,128)}), f32[64,512]{1,0:T(8,128)}) %reduce-scatter.8.cloned.1.call-update) | async-done | bytes 131088 | tf_op jit(solution)/shard_map/reduce_scatter | solution.py:70
  545.8 1.5 convert_element_type.79
  (16 shorter events, 0.1 us)
Async XLA Ops:
  7.2 3.9 copy-start.8
  7.2 4.1 copy-start.7
  7.2 44.1 %all-gather.5.cloned.1.call-start = ((), (), s32[]{:S(2)}) async-start(), calls=%async_computation.3 | async-start | bytes 1114112 | tf_op jit(solution)/shard_map/all_gather | solution.py:32
  7.9 82.5 %all-gather.7.cloned.1.call-start = ((), (), s32[]{:S(2)}) async-start(), calls=%async_computation.5 | async-start | bytes 1114112 | tf_op jit(solution)/shard_map/all_gather | solution.py:33
  8.7 225.5 %all-reduce.3.cloned.1.call-start = ((), (), s32[]{:S(2)}) async-start(), calls=%async_computation.10 | async-start | bytes 14680064 | tf_op jit(solution)/shard_map/psum | solution.py:38
  51.3 4.5 copy-start
  59.0 0.7 copy-start.9
  59.1 260.5 %reduce-scatter.10.cloned.1.call-start = ((), (), s32[]{:S(2)}) async-start(), calls=%async_computation.9 | async-start | bytes 3899392 | tf_op jit(solution)/shard_map/reduce_scatter | solution.py:53
  90.5 2.1 copy-start.5
  91.6 0.9 copy-start.1
  101.8 269.7 %all-gather.9.cloned.1.call-start = ((), (), s32[]{:S(2)}) async-start(), calls=%async_computation.6 | async-start | bytes 1949696 | tf_op jit(solution)/shard_map/all_gather | solution.py:61
  321.5 102.0 %all-gather.11.cloned.1.call-start = ((), (), s32[]{:S(2)}) async-start(), calls=%async_computation.7 | async-start | bytes 1949696 | tf_op jit(solution)/shard_map/all_gather | solution.py:62
  322.1 163.2 %reduce-scatter.6.cloned.1.call-start = ((), (), s32[]{:S(2)}) async-start(), calls=%async_computation.4 | async-start | bytes 2228224 | tf_op jit(solution)/shard_map/reduce_scatter | solution.py:43
  322.1 5.5 %copy-start.2 = (bf16[896,4,128]{2,1,0:T(4,128)(2,1)S(1)}, bf16[896,4,128]{2,1,0:T(4,128)(2,1)}, u32[]{:S(2)}) copy-start(bf16[896,4,128]{2,1,0:T(4,128)(2,1)} %copy-done.1) | copy-start | bytes 2752516
  322.2 5.5 copy-start.6
  326.4 1.3 copy-start.4
  330.3 215.5 %reduce-scatter.8.cloned.1.call-start = ((), (), s32[]{:S(2)}) async-start(), calls=%async_computation.8 | async-start | bytes 2228224 | tf_op jit(solution)/shard_map/reduce_scatter | solution.py:70
  428.2 1.2 copy-start.3
  429.4 4.1 copy-start.10
Sparse Core Ops, SparseCore 0:
  9.8 41.4 all-gather.4
  53.2 37.2 all-gather.6
  93.9 140.2 all-reduce.2
  238.1 81.3 reduce-scatter.9
  322.7 48.7 all-gather.8
  374.7 48.7 all-gather.10
  426.2 59.0 reduce-scatter.5
  488.0 57.7 reduce-scatter.7
where the time goes:
time: 555 us; the launch traced here: 554 us
  waiting for transfers between devices  483 us (87%)
  matrix products  31 us (6%)
  local copies, waits for them, and re-layouts  15.3 us (3%)
  between operations  14.3 us (3%)
  other arithmetic  10.1 us (2%)
    psum x1, waiting for transfers between devices, shards(): gate_full, up_full = lax.psum((part_gate, part_up), 'dp')  132 us
    reduce_scatter x1, waiting for transfers between devices, shards(): lax.psum_scatter(part_hidden, 'dp', scatter_dimension=0, tiled=True)  85.4 us
    reduce_scatter x1, waiting for transfers between devices, shards(): lax.psum_scatter(contract_cols(gate_grads_all, gate_eff) + contract_cols(...  59 us
    all_gather x1, waiting for transfers between devices, shards(): lax.all_gather(grad_up_act, 'dp', axis=0, tiled=True)  48 us
    reduce_scatter x1, waiting for transfers between devices, shards(): lax.psum_scatter(jnp.dot(hidden_all, down_eff, preferred_element_type=jnp...  45.4 us
    all_gather x1, waiting for transfers between devices, shards(): lax.all_gather(grad_gate_act, 'dp', axis=0, tiled=True)  41.2 us
    all_gather x1, waiting for transfers between devices, shards(): lax.all_gather(tokens, 'tensor', axis=0, tiled=True)  39.4 us
    all_gather x1, waiting for transfers between devices, shards(): lax.all_gather(grad_output, 'tensor', axis=0, tiled=True)  30.6 us
  transfers between devices with their start and end apart: 8, of which 8 were waited for; matrix products, arithmetic and copies ran while one was open for 9% of the time, Pallas kernels for 0%

commit v1 on v0

v1 whole, which is shorter than its diff:
```python
import jax
import jax.numpy as jnp
from jax import lax
from jax.experimental import pallas as pl
from jax.experimental.pallas import tpu as pltpu
from jax.sharding import PartitionSpec as P

BF = jnp.bfloat16
F32 = jnp.float32
SIDE = 128
RING = 4
DEPTH = 8
PHASE_DTYPES = (BF, F32)

FAR_R, OWN_R, SUM_R, FAR_L, OWN_L, SUM_L = range(6)


def mm(left, right_side, dims):
    return lax.dot_general(left, right_side, (dims, ((), ())), preferred_element_type=F32)


def kernel(
    tok_in, cot_in, wg_in, wu_in, wd_in, gmask, umask, dmask,
    o_out, gt_out, gg_out, gu_out, gd_out,
    rows, weights, weight_d, part, sent1, got1, acc1, sent2, got2, fin,
    acts, outs, peer, zsent, zgot, grads, grad_d, small,
    ag_s, ag_r, rs_s, rs_r, av_s, av_r, ex_s, ex_r, zr_s, zr_r, loc,
):
    dp = lax.axis_index("dp")
    tensor = lax.axis_index("tensor")
    x, y = dp // RING, dp % RING
    z, core = tensor // 2, tensor % 2
    sends = []

    def wrap(value, n):
        return lax.rem(value + 2 * n, n)

    def at(dx=0, dy=0, dz=0, dc=0):
        return {
            "dp": wrap(x + dx, RING) * RING + wrap(y + dy, RING),
            "tensor": wrap(z + dz, DEPTH) * 2 + (1 - core if dc else core),
        }

    def remote(src, dst, s_sem, r_sem, device):
        return pltpu.make_async_remote_copy(
            src_ref=src, dst_ref=dst, send_sem=s_sem, recv_sem=r_sem,
            device_id=device, device_id_type=pl.DeviceIdType.MESH,
        )

    def push(src, dst, s_sem, r_sem, device):
        copy = remote(src, dst, s_sem, r_sem, device)
        copy.start()
        sends.append(copy)

    def arrived(dst, s_sem, r_sem, device):
        remote(dst, dst, s_sem, r_sem, device).wait_recv()

    def block_rows(zz, cc):
        return pl.ds(pl.multiple_of((wrap(zz, DEPTH) * 2 + cc) * 64, 64), 64)

    mine = block_rows(z, core)
    loads = [
        pltpu.make_async_copy(tok_in, rows.at[0, mine], loc.at[0]),
        pltpu.make_async_copy(cot_in, rows.at[1, mine], loc.at[1]),
        pltpu.make_async_copy(wg_in, weights.at[0], loc.at[2]),
        pltpu.make_async_copy(wu_in, weights.at[1], loc.at[3]),
        pltpu.make_async_copy(wd_in, weight_d, loc.at[4]),
    ]
    for load in loads:
        load.start()

    barrier = pltpu.get_barrier_semaphore()
    peers = [at(dx=1), at(dx=-1), at(dy=1), at(dy=-1), at(dz=1), at(dz=-1), at(dc=1)]
    for device in peers:
        pl.semaphore_signal(barrier, inc=1, device_id=device, device_id_type=pl.DeviceIdType.MESH)
    pl.semaphore_wait(barrier, len(peers))

    def half(zz, cc, second):
        start = (wrap(zz, DEPTH) * 2 + cc) * 64 + 32 * second
        return pl.ds(pl.multiple_of(start, 32), 32)

    def z_push(i, slot, where, device):
        ref = rows.at[i, where]
        push(ref, ref, ag_s.at[i, slot], ag_r.at[i, slot], device)

    def z_arrived(i, slot, where, device):
        arrived(rows.at[i, where], ag_s.at[i, slot], ag_r.at[i, slot], device)

    up, down, other = at(dz=1), at(dz=-1), at(dc=1)

    def gather_start(i):
        loads[i].wait()
        z_push(i, 0, mine, up)
        z_push(i, 4, mine, down)
        z_push(i, 8, mine, other)

    def gather_step(i, k):
        if k < 4:
            z_arrived(i, k - 1, block_rows(z - k, core), up)
            if k < 3:
                z_push(i, k, block_rows(z - k, core), up)
            else:
                z_push(i, 3, half(z - 3, core, 0), up)
            z_push(i, 8 + 2 * k - 1, block_rows(z - k, core), other)
            z_arrived(i, 4 + k - 1, block_rows(z + k, core), down)
            if k < 3:
                z_push(i, 4 + k, block_rows(z + k, core), down)
            else:
                z_push(i, 7, half(z + 3, core, 1), down)
            z_push(i, 8 + 2 * k, block_rows(z + k, core), other)
        else:
            z_arrived(i, 3, half(z - 4, core, 0), up)
            z_arrived(i, 7, half(z + 4, core, 1), down)
            z_push(i, 15, block_rows(z + 4, core), other)

    def gather_end(i):
        z_arrived(i, 8, block_rows(z, 1 - core), other)
        for k in range(1, 4):
            z_arrived(i, 8 + 2 * k - 1, block_rows(z - k, 1 - core), other)
            z_arrived(i, 8 + 2 * k, block_rows(z + k, 1 - core), other)
        z_arrived(i, 15, block_rows(z + 4, 1 - core), other)

    gather_start(0)
    gather_start(1)

    def keep(mask, i, j):
        return mask[i, j].astype(F32)

    def mask_weight(ref, mask, n_rows, n_cols):
        def body(i, carry):
            rows_i = pl.ds(pl.multiple_of(i * SIDE, SIDE), SIDE)
            for j in range(n_cols):
                cols = pl.ds(j * SIDE, SIDE)
                ref[rows_i, cols] = (ref[rows_i, cols].astype(F32) * keep(mask, i, j)).astype(BF)
            return carry

        lax.fori_loop(0, n_rows, body, 0)

    for load in loads[2:]:
        load.wait()
    mask_weight(weights.at[0], gmask, 4, 7)
    gather_step(0, 1)
    gather_step(1, 1)
    mask_weight(weights.at[1], umask, 4, 7)
    gather_step(0, 2)
    gather_step(1, 2)
    mask_weight(weight_d, dmask, 7, 4)
    gather_step(0, 3)
    gather_step(1, 3)
    gather_step(0, 4)
    gather_step(1, 4)
    gather_end(0)

    def tiles(body, count=4):
        def step(i, carry):
            body(i, pl.ds(pl.multiple_of(i * 256, 256), 256))
            return carry

        lax.fori_loop(0, count, step, 0)

    def partial(a):
        def body(i, where):
            if a < 2:
                part[a, where] = mm(rows[0, where], weights[a], ((1,), (0,)))
            else:
                part[2, where] = mm(rows[1, where], weight_d[...], ((1,), (1,)))

        tiles(body)

    def ring(h, phase):
        if (h + phase) % 2 == 0:
            return x, at(dx=1), at(dx=-1)
        return y, at(dy=1), at(dy=-1)

    def rs_refs(a, h, phase):
        if phase == 0:
            return part.at[a], h * 512, 64, sent1.at[a, h], got1.at[a, h], acc1.at[a, h]
        return acc1.at[a, h], 0, 16, sent2.at[a, h], got2.at[a, h], fin.at[a, h]

    def rs_sem(sems, a, h, phase, slot):
        return sems.at[a, h, 6 * phase + slot]

    def rs_push(a, h, phase, slot, device):
        _, _, _, sent, got, _ = rs_refs(a, h, phase)
        push(
            sent.at[slot], got.at[slot],
            rs_sem(rs_s, a, h, phase, slot), rs_sem(rs_r, a, h, phase, slot), device,
        )

    def rs_arrived(a, h, phase, slot, device):
        _, _, _, _, got, _ = rs_refs(a, h, phase)
        arrived(
            got.at[slot], rs_sem(rs_s, a, h, phase, slot), rs_sem(rs_r, a, h, phase, slot), device
        )

    def rs_block(a, h, phase, d, second):
        src, base, n, _, _, _ = rs_refs(a, h, phase)
        start = base + 2 * n * d + n * second
        return src[pl.ds(pl.multiple_of(start, n), n), :]

    def rs_first(a, h, phase):
        q, right, left = ring(h, phase)
        sent = rs_refs(a, h, phase)[3]
        dtype = PHASE_DTYPES[phase]
        far, to_r, to_l = wrap(q + 2, RING), wrap(q + 1, RING), wrap(q - 1, RING)
        for slot, d, second, device in (
            (FAR_R, far, 0, right), (FAR_L, far, 1, left), (OWN_R, to_r, 1, right), (OWN_L, to_l, 0, left),
        ):
            sent[slot] = rs_block(a, h, phase, d, second).astype(dtype)
            rs_push(a, h, phase, slot, device)

    def rs_second(a, h, phase):
        q, right, left = ring(h, phase)
        _, _, _, sent, got, _ = rs_refs(a, h, phase)
        dtype = PHASE_DTYPES[phase]
        to_r, to_l = wrap(q + 1, RING), wrap(q - 1, RING)
        rs_arrived(a, h, phase, FAR_R, right)
        sent[SUM_R] = (rs_block(a, h, phase, to_r, 0) + got[FAR_R].astype(F32)).astype(dtype)
        rs_push(a, h, phase, SUM_R, right)
        rs_arrived(a, h, phase, FAR_L, left)
        sent[SUM_L] = (rs_block(a, h, phase, to_l, 1) + got[FAR_L].astype(F32)).astype(dtype)
        rs_push(a, h, phase, SUM_L, left)

    def rs_last(a, h, phase):
        q, right, left = ring(h, phase)
        _, _, n, _, got, dst = rs_refs(a, h, phase)
        rs_arrived(a, h, phase, OWN_R, right)
        rs_arrived(a, h, phase, OWN_L, left)
        rs_arrived(a, h, phase, SUM_R, right)
        rs_arrived(a, h, phase, SUM_L, left)
        dst[pl.ds(0, n), :] = (
            rs_block(a, h, phase, q, 0) + got[SUM_R].astype(F32) + got[OWN_L].astype(F32)
        )
        dst[pl.ds(n, n), :] = (
            rs_block(a, h, phase, q, 1) + got[OWN_R].astype(F32) + got[SUM_L].astype(F32)
        )

    def both(step, a, phase):
        for h in range(2):
            step(a, h, phase)

    def av_rows(h, phase, d, second=None):
        n = 32 if phase == 0 else 128
        start = h * 512 + 128 * ring(h, 0)[0] + 32 * d if phase == 0 else h * 512 + 128 * d
        if second is None:
            return pl.ds(pl.multiple_of(start, n), n)
        return pl.ds(pl.multiple_of(start + n // 2 * second, n // 2), n // 2)

    def av_move(a, h, phase, slot, where, device, send):
        ref = acts.at[a, where]
        sems = av_s.at[a, h, 4 * phase + slot], av_r.at[a, h, 4 * phase + slot]
        if send:
            push(ref, ref, *sems, device)
        else:
            arrived(ref, *sems, device)

    def av_first(a, h, phase):
        q, right, left = ring(h, 1 - phase)
        av_move(a, h, phase, 0, av_rows(h, phase, q), right, True)
        av_move(a, h, phase, 1, av_rows(h, phase, q), left, True)

    def av_second(a, h, phase):
        q, right, left = ring(h, 1 - phase)
        from_l, from_r = wrap(q - 1, RING), wrap(q + 1, RING)
        av_move(a, h, phase, 0, av_rows(h, phase, from_l), right, False)
        av_move(a, h, phase, 2, av_rows(h, phase, from_l, 0), right, True)
        av_move(a, h, phase, 1, av_rows(h, phase, from_r), left, False)
        av_move(a, h, phase, 3, av_rows(h, phase, from_r, 1), left, True)

    def av_last(a, h, phase):
        q, right, left = ring(h, 1 - phase)
        far = wrap(q + 2, RING)
        av_move(a, h, phase, 2, av_rows(h, phase, far, 0), right, False)
        av_move(a, h, phase, 3, av_rows(h, phase, far, 1), left, False)

    def own_rows(h):
        return av_rows(h, 0, ring(h, 1)[0])

    def exchange(b):
        push(outs.at[b, :, 1 - core], peer.at[b], ex_s.at[b], ex_r.at[b], other)

    def exchanged(b):
        arrived(peer.at[b], ex_s.at[b], ex_r.at[b], other)

    def chip_sum(b, zz):
        return outs[b, wrap(zz, DEPTH), core] + peer[b, wrap(zz, DEPTH)]

    def zr_move(b, way, k, send):
        where = pl.ds(0, 64) if k < 4 else pl.ds(32 * way, 32)
        sems = zr_s.at[b, way, k - 1], zr_r.at[b, way, k - 1]
        device = (up, down)[way]
        if send:
            push(zsent.at[b, way, k - 1, where], zgot.at[b, way, k - 1, where], *sems, device)
        else:
            arrived(zgot.at[b, way, k - 1, where], *sems, device)

    def zr_step(b, k):
        for way in range(2):
            target = z + k if way == 0 else z - k
            if k == 4:
                where = pl.ds(32 * way, 32)
                wrapped = wrap(target, DEPTH)
                zsent[b, way, 3, where] = outs[b, wrapped, core, where] + peer[b, wrapped, where]
            else:
                zr_move(b, way, k + 1, False)
                total = chip_sum(b, target)
                if k == 3:
                    fresh, rest = pl.ds(32 * way, 32), pl.ds(32 - 32 * way, 32)
                    zsent[b, way, 2] = total
                    zsent[b, way, 2, fresh] = zsent[b, way, 2, fresh] + zgot[b, way, 3, fresh]
                else:
                    zsent[b, way, k - 1] = total + zgot[b, way, k]
            zr_move(b, way, k, True)

    def zr_last(b, out):
        zr_move(b, 0, 1, False)
        zr_move(b, 1, 1, False)
        small[b] = (chip_sum(b, z) + zgot[b, 0, 0] + zgot[b, 1, 0]).astype(BF)
        pltpu.make_async_copy(small.at[b], out, loc.at[5 + b]).start()

    def store(out, src, i):
        pltpu.make_async_copy(src, out, loc.at[i]).start()

    def grad_weights():
        def body(i, where):
            left = rows[0, :, where].T
            for a, mask in ((0, gmask), (1, umask)):
                tile = mm(left, acts[1 + a], ((1,), (0,)))
                for r in range(2):
                    for j in range(7):
                        cols = slice(j * SIDE, (j + 1) * SIDE)
                        out_rows = pl.ds(pl.multiple_of(i * 256 + r * SIDE, SIDE), SIDE)
                        grads[a, out_rows, cols] = (
                            tile[r * SIDE : (r + 1) * SIDE, cols] * keep(mask, 2 * i + r, j)
                        ).astype(BF)

        tiles(body, 2)

    def grad_down():
        def step(i, carry):
            where = pl.ds(pl.multiple_of(i * SIDE, SIDE), SIDE)
            tile = mm(acts[0, :, where].T, rows[1], ((1,), (0,)))
            for j in range(4):
                cols = slice(j * SIDE, (j + 1) * SIDE)
                grad_d[where, cols] = (tile[:, cols] * keep(dmask, i, j)).astype(BF)
            return carry

        lax.fori_loop(0, 7, step, 0)

    partial(0)
    both(rs_first, 0, 0)
    partial(1)
    both(rs_first, 1, 0)
    gather_end(1)
    partial(2)
    both(rs_second, 0, 0)
    both(rs_first, 2, 0)
    both(rs_second, 1, 0)
    both(rs_last, 0, 0)
    both(rs_first, 0, 1)
    both(rs_second, 2, 0)
    both(rs_last, 1, 0)
    both(rs_first, 1, 1)
    both(rs_second, 0, 1)
    both(rs_second, 1, 1)
    both(rs_last, 2, 0)
    both(rs_first, 2, 1)
    both(rs_last, 0, 1)
    both(rs_last, 1, 1)
    for h in range(2):
        gate = fin[0, h]
        acts[0, own_rows(h)] = (gate * jax.nn.sigmoid(gate) * fin[1, h]).astype(BF)
        av_first(0, h, 0)
    both(rs_second, 2, 1)
    both(av_second, 0, 0)
    both(rs_last, 2, 1)
    for h in range(2):
        gate, upv, grad = fin[0, h], fin[1, h], fin[2, h]
        s = jax.nn.sigmoid(gate)
        acts[1, own_rows(h)] = (grad * upv * s * (1.0 + gate * (1.0 - s))).astype(BF)
        acts[2, own_rows(h)] = (grad * (gate * s)).astype(BF)
        av_first(1, h, 0)
        av_first(2, h, 0)
    both(av_last, 0, 0)
    both(av_first, 0, 1)
    both(av_second, 1, 0)
    both(av_second, 2, 0)
    both(av_last, 1, 0)
    both(av_first, 1, 1)
    both(av_second, 0, 1)
    both(av_last, 2, 0)
    both(av_first, 2, 1)
    both(av_last, 0, 1)

    def output_part(i, where):
        tile = mm(acts[0, where], weight_d[...], ((1,), (0,)))
        outs[0, pl.ds(2 * i, 2)] = tile.reshape(2, 2, 64, 512)

    tiles(output_part)
    exchange(0)
    both(av_second, 1, 1)
    exchanged(0)
    zr_step(0, 4)
    both(av_second, 2, 1)
    zr_step(0, 3)
    both(av_last, 1, 1)
    zr_step(0, 2)
    grad_down()
    store(gd_out, grad_d, 7)
    zr_step(0, 1)
    both(av_last, 2, 1)

    def tokens_part(i, where):
        tile = mm(acts[1, where], weights[0], ((1,), (1,))) + mm(acts[2, where], weights[1], ((1,), (1,)))
        outs[1, pl.ds(2 * i, 2)] = tile.reshape(2, 2, 64, 512)

    tiles(tokens_part)
    exchange(1)
    zr_last(0, o_out)
    exchanged(1)
    zr_step(1, 4)
    grad_weights()
    store(gg_out, grads.at[0], 8)
    store(gu_out, grads.at[1], 9)
    zr_step(1, 3)
    zr_step(1, 2)
    zr_step(1, 1)
    zr_last(1, gt_out)

    pltpu.make_async_copy(small.at[0], o_out, loc.at[5]).wait()
    pltpu.make_async_copy(small.at[1], gt_out, loc.at[6]).wait()
    pltpu.make_async_copy(grad_d, gd_out, loc.at[7]).wait()
    pltpu.make_async_copy(grads.at[0], gg_out, loc.at[8]).wait()
    pltpu.make_async_copy(grads.at[1], gu_out, loc.at[9]).wait()
    for copy in sends:
        copy.wait_send()


def shards(*args):
    anywhere = pl.BlockSpec(memory_space=pl.ANY)
    scalars = pl.BlockSpec(memory_space=pltpu.SMEM)
    dma = pltpu.SemaphoreType.DMA
    d1, d2 = PHASE_DTYPES
    return tuple(
        pl.pallas_call(
            kernel,
            out_shape=[
                jax.ShapeDtypeStruct((64, 512), BF),
                jax.ShapeDtypeStruct((64, 512), BF),
                jax.ShapeDtypeStruct((512, 896), BF),
                jax.ShapeDtypeStruct((512, 896), BF),
                jax.ShapeDtypeStruct((896, 512), BF),
            ],
            in_specs=[anywhere] * 5 + [scalars] * 3,
            out_specs=[anywhere] * 5,
            scratch_shapes=[
                pltpu.VMEM((2, 1024, 512), BF),
                pltpu.VMEM((2, 512, 896), BF),
                pltpu.VMEM((896, 512), BF),
                pltpu.VMEM((3, 1024, 896), F32),
                pltpu.VMEM((3, 2, 6, 64, 896), d1),
                pltpu.VMEM((3, 2, 6, 64, 896), d1),
                pltpu.VMEM((3, 2, 128, 896), F32),
                pltpu.VMEM((3, 2, 6, 16, 896), d2),
                pltpu.VMEM((3, 2, 6, 16, 896), d2),
                pltpu.VMEM((3, 2, 32, 896), F32),
                pltpu.VMEM((3, 1024, 896), BF),
                pltpu.VMEM((2, 8, 2, 64, 512), F32),
                pltpu.VMEM((2, 8, 64, 512), F32),
                pltpu.VMEM((2, 2, 4, 64, 512), F32),
                pltpu.VMEM((2, 2, 4, 64, 512), F32),
                pltpu.VMEM((2, 512, 896), BF),
                pltpu.VMEM((896, 512), BF),
                pltpu.VMEM((2, 64, 512), BF),
                dma((2, 16)), dma((2, 16)),
                dma((3, 2, 12)), dma((3, 2, 12)),
                dma((3, 2, 8)), dma((3, 2, 8)),
                dma((2,)), dma((2,)),
                dma((2, 2, 4)), dma((2, 2, 4)),
                dma((10,)),
            ],
            compiler_params=pltpu.CompilerParams(
                collective_id=0, has_side_effects=True, vmem_limit_bytes=64_000_000
            ),
            name="ffn",
        )(*args)
    )


def solution(mesh):
    return jax.shard_map(
        shards,
        mesh=mesh,
        in_specs=(
            P("tensor", "dp"),
            P("tensor", "dp"),
            P("dp", "tensor"),
            P("dp", "tensor"),
            P("tensor", "dp"),
            P("dp", "tensor"),
            P("dp", "tensor"),
            P("tensor", "dp"),
        ),
        out_specs=(
            P("tensor", "dp"),
            P("tensor", "dp"),
            P("dp", "tensor"),
            P("dp", "tensor"),
            P("tensor", "dp"),
        ),
        check_vma=False,
    )
```

time: 555 us -> 136 us (0.25)
  waiting for transfers between devices: 483 us -> 0 us
  Pallas kernels: 0 us -> 126 us
  matrix products: 31 us -> 0 us
  between operations: 14.3 us -> 0.65 us
  other arithmetic: 10.1 us -> 0 us
  local copies, waits for them, and re-layouts: 15.3 us -> 8.18 us
    reduce_scatter x3 -> x0, waiting for transfers between devices: 190 us -> none  [the longest x1 85.4 us: shards(): lax.psum_scatter(part_hidden, 'dp', scatter_dimension=0, tiled=True)]
    all_gather x4 -> x0, waiting for transfers between devices: 159 us -> none  [the longest x1 48 us: shards(): lax.all_gather(grad_up_act, 'dp', axis=0, tiled=True)]
    psum x1 -> x0, waiting for transfers between devices: 132 us -> none  [shards(): gate_full, up_full = lax.psum((part_gate, part_up), 'dp')]
    pallas_call x0 -> x1, Pallas kernels: none -> 126 us  [shards(): pl.pallas_call(kernel, out_shape=[jax.ShapeDtypeStruct((64, 512), BF), ja...]
    dot_general x9 -> x0, matrix products: 31 us -> none  [the longest x3 12.9 us: contract_cols(): lax.dot_general(left, right_side, (((1,), (1,)), ((), ())), preferred_ele...]
    convert_element_type x7 -> x0, other arithmetic: 10 us -> none  [the longest x1 4.26 us: shards(): (gate_full * jax.nn.sigmoid(gate_full) * up_full).astype(jnp.bfloat16)]
    unnamed x31 -> x12, local copies, waits for them, and re-layouts: 13.7 us -> 8.18 us
  transfers between devices with their start and end apart: 8 -> 0, of which waited for: 8 -> 0; matrix products, arithmetic and copies ran while one was open for 9% -> 0% of each run, Pallas kernels for 0% -> 0%
where the time goes in v1:
time: 136 us; the launch traced here: 135 us
  Pallas kernels  126 us (93%)
  local copies, waits for them, and re-layouts  8.18 us (6%)
    pallas_call x1, Pallas kernels, shards(): pl.pallas_call(kernel, out_shape=[jax.ShapeDtypeStruct((64, 512), BF), ja...  126 us
    unnamed x12, local copies, waits for them, and re-layouts  8.18 us

profile of v1, /device:TPU:8, one launch (start us, length us, event | category | flops | bytes accessed | tf_op | source)
XLA Modules:
  0.0 135.2 jit_solution(1524108976719475666)
XLA Ops:
  0.6 1.4 %copy.13.dmask = s32[7,4]{1,0:T(8,128)} copy(s32[7,4]{0,1:T(4,128)} %param.15) | data formatting | bytes 224 | tf_op args[7]
  2.0 126.4 %ffn.1 = (bf16[64,512]{1,0:T(8,128)(2,1)}, bf16[64,512]{1,0:T(8,128)(2,1)}, bf16[512,896]{1,0:T(8,128)(2,1)}, bf16[512,896]{1,0:T(8,128)(2,1)}, bf16[896,512]{1,0:T(8,128)(2,1)}) custom-call(bf16[64,512]{1,0:T(8,128)(2,1)} %tok_in.1, bf16[64,512]{1,0:T(8,128)(2,1)} %cot_in.1, bf16[512,896]{1,0:T(8,128)(2,1)} %wg_in.1, bf16[512,896]{1,0:T(8,128)(2,1)} %wu_in.1, ...), custom_call_target="tpu_custom_call" | custom-call | tf_op jit(solution)/shard_map/ffn/pallas_call | solution.py:445
  128.4 0.0 copy-start.2
  128.4 1.5 %copy.19 = bf16[64,512]{1,0:T(8,128)(2,1)} copy(bf16[64,512]{1,0:T(8,128)(2,1)} %get-tuple-element.10) | data formatting | bytes 131072
  129.9 0.0 copy-done.2
  129.9 0.6 copy.20
  130.5 0.0 copy-start.1
  130.5 2.3 %copy.21 = bf16[512,896]{1,0:T(8,128)(2,1)} copy(bf16[512,896]{1,0:T(8,128)(2,1)} %get-tuple-element.12) | data formatting | bytes 1835008
  132.8 0.0 copy-done.1
  132.8 0.0 copy-start
  132.8 0.9 copy.22
  133.7 0.6 copy-done
  134.3 0.9 copy.23
Async XLA Ops:
  128.4 1.5 %copy-start.2 = (bf16[64,512]{1,0:T(8,128)(2,1)S(1)}, bf16[64,512]{1,0:T(8,128)(2,1)}, u32[]{:S(2)}) copy-start(bf16[64,512]{1,0:T(8,128)(2,1)} %get-tuple-element.11) | copy-start | bytes 196612
  130.5 2.3 %copy-start.1 = (bf16[512,896]{1,0:T(8,128)(2,1)S(1)}, bf16[512,896]{1,0:T(8,128)(2,1)}, u32[]{:S(2)}) copy-start(bf16[512,896]{1,0:T(8,128)(2,1)} %get-tuple-element.13) | copy-start | bytes 2752516
  132.8 1.5 %copy-start = (bf16[896,512]{1,0:T(8,128)(2,1)S(1)}, bf16[896,512]{1,0:T(8,128)(2,1)}, u32[]{:S(2)}) copy-start(bf16[896,512]{1,0:T(8,128)(2,1)} %get-tuple-element.14) | copy-start | bytes 2752516

commit v2 on v0

v2 whole, which is shorter than its diff:
```python
import jax
import jax.numpy as jnp
from jax import lax
from jax.experimental import pallas as pl
from jax.experimental.pallas import tpu as pltpu
from jax.sharding import PartitionSpec as P

BF = jnp.bfloat16
F32 = jnp.float32
SIDE = 128
RING = 4
DEPTH = 8
CHUNKS = 2
OWN = 64 // CHUNKS
MANY = 1024 // CHUNKS
PIECE = 256
PHASE_DTYPES = (BF, F32)

FAR_R, OWN_R, SUM_R, FAR_L, OWN_L, SUM_L = range(6)

SCHEDULE = (
    ("G", 0, 0),
    ("G", 1, 0),
    ("M", 1),
    ("M", 0),
    ("M", 2),
    ("N", 0, 0, 1),
    ("N", 0, 0, 7),
    ("N", 0, 0, 2),
    ("N", 0, 0, 6),
    ("N", 1, 0, 1),
    ("N", 1, 0, 7),
    ("N", 1, 0, 2),
    ("N", 1, 0, 6),
    ("G", 0, 1),
    ("N", 0, 0, 3),
    ("N", 0, 0, 5),
    ("N", 0, 0, 4),
    ("E", 0, 0),
    ("P", 0, 0),
    ("F", 0, 0, 0, 0),
    ("N", 1, 0, 3),
    ("N", 1, 0, 5),
    ("F", 0, 0, 1, 0),
    ("N", 1, 0, 4),
    ("P", 1, 0),
    ("F", 1, 0, 0, 0),
    ("F", 1, 0, 1, 0),
    ("N", 0, 1, 1),
    ("N", 0, 1, 7),
    ("N", 0, 1, 2),
    ("N", 0, 1, 6),
    ("G", 1, 1),
    ("E", 1, 0),
    ("P", 2, 0),
    ("F", 2, 0, 0, 0),
    ("F", 2, 0, 1, 0),
    ("S", 0, 0, 0, 0),
    ("S", 0, 0, 1, 0),
    ("S", 1, 0, 0, 0),
    ("N", 0, 1, 3),
    ("N", 0, 1, 5),
    ("S", 1, 0, 1, 0),
    ("N", 0, 1, 4),
    ("E", 0, 1),
    ("P", 0, 1),
    ("N", 1, 1, 1),
    ("N", 1, 1, 2),
    ("N", 1, 1, 6),
    ("F", 0, 1, 0, 0),
    ("F", 0, 1, 1, 0),
    ("N", 1, 1, 7),
    ("S", 2, 0, 0, 0),
    ("S", 2, 0, 1, 0),
    ("P", 1, 1),
    ("F", 1, 1, 0, 0),
    ("F", 1, 1, 1, 0),
    ("L", 0, 0, 0, 0),
    ("F", 0, 0, 0, 1),
    ("L", 0, 0, 1, 0),
    ("F", 0, 0, 1, 1),
    ("L", 1, 0, 0, 0),
    ("F", 1, 0, 0, 1),
    ("L", 1, 0, 1, 0),
    ("F", 1, 0, 1, 1),
    ("S", 0, 1, 0, 0),
    ("S", 0, 1, 1, 0),
    ("N", 1, 1, 3),
    ("N", 1, 1, 4),
    ("N", 1, 1, 5),
    ("L", 2, 0, 0, 0),
    ("F", 2, 0, 0, 1),
    ("E", 1, 1),
    ("L", 2, 0, 1, 0),
    ("F", 2, 0, 1, 1),
    ("P", 2, 1),
    ("F", 2, 1, 0, 0),
    ("F", 2, 1, 1, 0),
    ("S", 1, 1, 0, 0),
    ("S", 1, 1, 1, 0),
    ("S", 0, 0, 1, 1),
    ("S", 0, 0, 0, 1),
    ("S", 1, 0, 1, 1),
    ("S", 1, 0, 0, 1),
    ("L", 0, 1, 0, 0),
    ("F", 0, 1, 0, 1),
    ("L", 0, 1, 1, 0),
    ("F", 0, 1, 1, 1),
    ("S", 2, 0, 1, 1),
    ("S", 2, 0, 0, 1),
    ("S", 2, 1, 0, 0),
    ("S", 2, 1, 1, 0),
    ("L", 1, 1, 0, 0),
    ("F", 1, 1, 0, 1),
    ("L", 1, 1, 1, 0),
    ("F", 1, 1, 1, 1),
    ("L", 0, 0, 1, 1),
    ("L", 0, 0, 0, 1),
    ("L", 1, 0, 1, 1),
    ("H", 0, 1),
    ("L", 1, 0, 0, 1),
    ("H", 0, 0),
    ("S", 0, 1, 1, 1),
    ("S", 0, 1, 0, 1),
    ("L", 2, 0, 1, 1),
    ("Q", 0, 1),
    ("L", 2, 0, 0, 1),
    ("Q", 0, 0),
    ("L", 2, 1, 0, 0),
    ("F", 2, 1, 0, 1),
    ("L", 2, 1, 1, 0),
    ("F", 2, 1, 1, 1),
    ("S", 1, 1, 1, 1),
    ("S", 1, 1, 0, 1),
    ("B", 0, 0, 1, 0),
    ("B", 0, 0, 0, 0),
    ("L", 0, 1, 1, 1),
    ("L", 0, 1, 0, 1),
    ("B", 1, 0, 1, 0),
    ("B", 1, 0, 0, 0),
    ("B", 2, 0, 1, 0),
    ("B", 2, 0, 0, 0),
    ("S", 2, 1, 1, 1),
    ("S", 2, 1, 0, 1),
    ("L", 1, 1, 1, 1),
    ("H", 1, 1),
    ("L", 1, 1, 0, 1),
    ("H", 1, 0),
    ("C", 0, 0, 1, 0),
    ("A", 0, 0, 1, 1),
    ("C", 0, 0, 0, 0),
    ("A", 0, 0, 0, 1),
    ("C", 1, 0, 1, 0),
    ("A", 1, 0, 1, 1),
    ("C", 1, 0, 0, 0),
    ("A", 1, 0, 0, 1),
    ("C", 2, 0, 1, 0),
    ("A", 2, 0, 1, 1),
    ("C", 2, 0, 0, 0),
    ("A", 2, 0, 0, 1),
    ("L", 2, 1, 1, 1),
    ("Q", 1, 1),
    ("L", 2, 1, 0, 1),
    ("Q", 1, 0),
    ("B", 0, 1, 1, 0),
    ("B", 0, 1, 0, 0),
    ("B", 0, 0, 0, 1),
    ("B", 0, 0, 1, 1),
    ("B", 1, 0, 0, 1),
    ("B", 1, 0, 1, 1),
    ("B", 2, 0, 0, 1),
    ("B", 2, 0, 1, 1),
    ("B", 1, 1, 1, 0),
    ("B", 1, 1, 0, 0),
    ("B", 2, 1, 1, 0),
    ("B", 2, 1, 0, 0),
    ("C", 0, 1, 1, 0),
    ("A", 0, 1, 1, 1),
    ("C", 0, 1, 0, 0),
    ("A", 0, 1, 0, 1),
    ("C", 0, 0, 0, 1),
    ("C", 0, 0, 1, 1),
    ("T", 0, 0, 0, 0),
    ("T", 0, 0, 0, 1),
    ("C", 1, 0, 0, 1),
    ("C", 1, 0, 1, 1),
    ("T", 1, 1, 0, 0),
    ("T", 1, 1, 0, 1),
    ("C", 2, 0, 0, 1),
    ("C", 1, 1, 1, 0),
    ("A", 1, 1, 1, 1),
    ("Z", 0, 0, 0, 4),
    ("C", 1, 1, 0, 0),
    ("A", 1, 1, 0, 1),
    ("C", 2, 0, 1, 1),
    ("T", 1, 2, 0, 0),
    ("T", 1, 2, 0, 1),
    ("C", 2, 1, 1, 0),
    ("A", 2, 1, 1, 1),
    ("C", 2, 1, 0, 0),
    ("A", 2, 1, 0, 1),
    ("Z", 0, 0, 1, 4),
    ("Z", 1, 0, 0, 4),
    ("B", 0, 1, 0, 1),
    ("B", 0, 1, 1, 1),
    ("Z", 1, 0, 1, 4),
    ("Z", 0, 0, 0, 3),
    ("Z", 0, 0, 1, 3),
    ("B", 1, 1, 1, 1),
    ("B", 1, 1, 0, 1),
    ("Z", 1, 0, 0, 3),
    ("Z", 1, 0, 1, 3),
    ("B", 2, 1, 1, 1),
    ("Z", 0, 0, 0, 2),
    ("B", 2, 1, 0, 1),
    ("Z", 0, 0, 1, 2),
    ("C", 0, 1, 1, 1),
    ("C", 0, 1, 0, 1),
    ("T", 0, 0, 1, 0),
    ("T", 0, 0, 1, 1),
    ("D", 0),
    ("Z", 1, 0, 0, 2),
    ("C", 1, 1, 1, 1),
    ("D", 1),
    ("C", 1, 1, 0, 1),
    ("T", 1, 1, 1, 0),
    ("T", 1, 1, 1, 1),
    ("W", 0, 1),
    ("Z", 0, 0, 0, 1),
    ("Z", 0, 1, 0, 4),
    ("Z", 1, 0, 1, 2),
    ("W", 0, 0),
    ("Z", 0, 0, 1, 1),
    ("C", 2, 1, 0, 1),
    ("C", 2, 1, 1, 1),
    ("T", 1, 2, 1, 0),
    ("T", 1, 2, 1, 1),
    ("W", 1, 0),
    ("W", 1, 1),
    ("Z", 0, 1, 1, 4),
    ("D", 2),
    ("Z", 1, 0, 0, 1),
    ("D", 3),
    ("Z", 1, 1, 0, 4),
    ("Y", 0, 0, 0),
    ("Z", 1, 1, 1, 4),
    ("Z", 0, 1, 0, 3),
    ("Z", 1, 0, 1, 1),
    ("Y", 0, 0, 1),
    ("Z", 0, 1, 1, 3),
    ("Y", 1, 0, 0),
    ("Z", 1, 1, 0, 3),
    ("Z", 1, 1, 1, 3),
    ("Z", 0, 1, 0, 2),
    ("Y", 1, 0, 1),
    ("Z", 0, 1, 1, 2),
    ("Z", 1, 1, 0, 2),
    ("Z", 1, 1, 1, 2),
    ("Z", 0, 1, 0, 1),
    ("Z", 0, 1, 1, 1),
    ("Z", 1, 1, 0, 1),
    ("Z", 1, 1, 1, 1),
    ("Y", 0, 1, 0),
    ("Y", 0, 1, 1),
    ("Y", 1, 1, 0),
    ("Y", 1, 1, 1),
)


def mm(left, right_side, dims):
    return lax.dot_general(left, right_side, (dims, ((), ())), preferred_element_type=F32)


def kernel(
    tok_in, cot_in, wg_in, wu_in, wd_in, gm_in, um_in, dm_in,
    o_out, gt_out, gg_out, gu_out, gd_out,
    rows, weights, weight_d, part, sent1, got1, acc1, sent2, got2, fin,
    acts, outs, peer, zsent, zgot, gmask, umask, dmask,
    ag_s, ag_r, rs_s, rs_r, av_s, av_r, ex_s, ex_r, zr_s, zr_r, loc,
):
    dp = lax.axis_index("dp")
    tensor = lax.axis_index("tensor")
    x, y = dp // RING, dp % RING
    z, core = tensor // 2, tensor % 2
    sends = []

    def wrap(value, n):
        return lax.rem(value + 2 * n, n)

    def at(dx=0, dy=0, dz=0, dc=0):
        return {
            "dp": wrap(x + dx, RING) * RING + wrap(y + dy, RING),
            "tensor": wrap(z + dz, DEPTH) * 2 + (1 - core if dc else core),
        }

    def remote(src, dst, s_sem, r_sem, device):
        return pltpu.make_async_remote_copy(
            src_ref=src, dst_ref=dst, send_sem=s_sem, recv_sem=r_sem,
            device_id=device, device_id_type=pl.DeviceIdType.MESH,
        )

    def push(src, dst, s_sem, r_sem, device):
        copy = remote(src, dst, s_sem, r_sem, device)
        copy.start()
        sends.append(copy)

    def arrived(dst, s_sem, r_sem, device):
        remote(dst, dst, s_sem, r_sem, device).wait_recv()

    def block_rows(zz, cc):
        return pl.ds(pl.multiple_of((wrap(zz, DEPTH) * 2 + cc) * OWN, OWN), OWN)

    mine, mine_there = block_rows(z, core), block_rows(z, 1 - core)
    row_loads = [
        [
            pltpu.make_async_copy(
                ref.at[pl.ds(OWN * k, OWN)], rows.at[i, k, mine], loc.at[CHUNKS * i + k]
            )
            for k in range(CHUNKS)
        ]
        for i, ref in enumerate((tok_in, cot_in))
    ]
    other_loads = [
        pltpu.make_async_copy(src, dst, loc.at[2 * CHUNKS + n])
        for n, (src, dst) in enumerate(
            (
                (gm_in, gmask), (um_in, umask), (dm_in, dmask),
                (wg_in, weights.at[0]), (wu_in, weights.at[1]), (wd_in, weight_d),
            )
        )
    ]
    for load in row_loads[0] + row_loads[1] + other_loads:
        load.start()

    barrier = pltpu.get_barrier_semaphore()
    peers = [at(dx=1), at(dx=-1), at(dy=1), at(dy=-1), at(dc=1)]
    peers += [at(dz=d) for d in (1, -1, 2, -2)]
    for device in peers:
        pl.semaphore_signal(barrier, inc=1, device_id=device, device_id_type=pl.DeviceIdType.MESH)
    pl.semaphore_wait(barrier, len(peers))

    def z_push(i, k, slot, where, device):
        ref = rows.at[i, k, where]
        push(ref, ref, ag_s.at[i, k, slot], ag_r.at[i, k, slot], device)

    def z_arrived(i, k, slot, where, device):
        arrived(rows.at[i, k, where], ag_s.at[i, k, slot], ag_r.at[i, k, slot], device)

    up, down, other = at(dz=1), at(dz=-1), at(dc=1)

    def half(zz, second):
        start = (wrap(zz, DEPTH) * 2 + core) * OWN + OWN // 2 * second
        return pl.ds(pl.multiple_of(start, OWN // 2), OWN // 2)

    def gather_start(i, k):
        row_loads[i][k].wait()
        z_push(i, k, 8, mine, other)
        for d in (2, -2, 1, -1):
            z_push(i, k, d % DEPTH, mine, at(dz=d))

    def gather_step(i, k, d):
        if d == 4:
            z_arrived(i, k, 4, half(z - 4, 0), up)
            z_arrived(i, k, 0, half(z - 4, 1), up)
            z_push(i, k, 12, block_rows(z - 4, core), other)
            return
        n = d if d < 4 else d - DEPTH
        sign = 1 if n > 0 else -1
        z_arrived(i, k, d, block_rows(z - n, core), up)
        if n == sign:
            z_push(i, k, 3 * sign % DEPTH, block_rows(z - n, core), at(dz=2 * sign))
        elif n == 2 * sign:
            z_push(i, k, 4 if n > 0 else 0, half(z - n, 0 if n > 0 else 1), at(dz=2 * sign))
        z_push(i, k, 8 + d, block_rows(z - n, core), other)

    def gather_end(i, k):
        z_arrived(i, k, 8, mine_there, other)
        for d in range(1, DEPTH):
            z_arrived(i, k, 8 + d, block_rows(z - d, 1 - core), other)

    def keep(mask, i, j):
        return mask[i, j].astype(F32)

    def mask_weight(n):
        for load in (other_loads[n], other_loads[3 + n]):
            load.wait()
        ref = weight_d if n == 2 else weights.at[n]
        n_rows, n_cols = (7, 4) if n == 2 else (4, 7)

        def body(i, carry):
            rows_i = pl.ds(pl.multiple_of(i * SIDE, SIDE), SIDE)
            for j in range(n_cols):
                cols = pl.ds(j * SIDE, SIDE)
                factor = keep(dmask, j, i) if n == 2 else keep((gmask, umask)[n], i, j)
                ref[rows_i, cols] = (ref[rows_i, cols].astype(F32) * factor).astype(BF)
            return carry

        lax.fori_loop(0, n_rows, body, 0)

    def tiles(body):
        def step(i, carry):
            body(i, pl.ds(pl.multiple_of(i * 256, 256), 256))
            return carry

        lax.fori_loop(0, MANY // 256, step, 0)

    def partial(a, k):
        def body(i, where):
            if a < 2:
                part[a, k, where] = mm(rows[0, k, where], weights[a], ((1,), (0,)))
            else:
                part[2, k, where] = mm(rows[1, k, where], weight_d[...], ((1,), (1,)))

        tiles(body)

    def ring(h, phase):
        if (h + phase) % 2 == 0:
            return x, at(dx=1), at(dx=-1)
        return y, at(dy=1), at(dy=-1)

    def rs_refs(a, k, h, phase):
        if phase == 0:
            return (
                part.at[a, k], h * (MANY // 2), MANY // 16,
                sent1.at[a, k, h], got1.at[a, k, h], acc1.at[a, k, h],
            )
        return acc1.at[a, k, h], 0, MANY // 64, sent2.at[a, k, h], got2.at[a, k, h], fin.at[a, k, h]

    def rs_sems(a, k, h, phase, slot):
        return rs_s.at[a, k, h, 6 * phase + slot], rs_r.at[a, k, h, 6 * phase + slot]

    def rs_push(a, k, h, phase, slot, device):
        _, _, _, sent, got, _ = rs_refs(a, k, h, phase)
        push(sent.at[slot], got.at[slot], *rs_sems(a, k, h, phase, slot), device)

    def rs_arrived(a, k, h, phase, slot, device):
        got = rs_refs(a, k, h, phase)[4]
        arrived(got.at[slot], *rs_sems(a, k, h, phase, slot), device)

    def rs_block(a, k, h, phase, d, second):
        src, base, n, _, _, _ = rs_refs(a, k, h, phase)
        start = base + 2 * n * d + n * second
        return src[pl.ds(pl.multiple_of(start, n), n), :]

    def rs_first(a, k, h, phase):
        q, right, left = ring(h, phase)
        sent = rs_refs(a, k, h, phase)[3]
        dtype = PHASE_DTYPES[phase]
        far, to_r, to_l = wrap(q + 2, RING), wrap(q + 1, RING), wrap(q - 1, RING)
        for slot, d, second, device in (
            (FAR_R, far, 0, right), (FAR_L, far, 1, left), (OWN_R, to_r, 1, right), (OWN_L, to_l, 0, left),
        ):
            sent[slot] = rs_block(a, k, h, phase, d, second).astype(dtype)
            rs_push(a, k, h, phase, slot, device)

    def rs_second(a, k, h, phase):
        q, right, left = ring(h, phase)
        _, _, _, sent, got, _ = rs_refs(a, k, h, phase)
        dtype = PHASE_DTYPES[phase]
        to_r, to_l = wrap(q + 1, RING), wrap(q - 1, RING)
        rs_arrived(a, k, h, phase, FAR_R, right)
        sent[SUM_R] = (rs_block(a, k, h, phase, to_r, 0) + got[FAR_R].astype(F32)).astype(dtype)
        rs_push(a, k, h, phase, SUM_R, right)
        rs_arrived(a, k, h, phase, FAR_L, left)
        sent[SUM_L] = (rs_block(a, k, h, phase, to_l, 1) + got[FAR_L].astype(F32)).astype(dtype)
        rs_push(a, k, h, phase, SUM_L, left)

    def rs_last(a, k, h, phase):
        q, right, left = ring(h, phase)
        _, _, n, _, got, dst = rs_refs(a, k, h, phase)
        rs_arrived(a, k, h, phase, OWN_R, right)
        rs_arrived(a, k, h, phase, OWN_L, left)
        rs_arrived(a, k, h, phase, SUM_R, right)
        rs_arrived(a, k, h, phase, SUM_L, left)
        dst[pl.ds(0, n), :] = (
            rs_block(a, k, h, phase, q, 0) + got[SUM_R].astype(F32) + got[OWN_L].astype(F32)
        )
        dst[pl.ds(n, n), :] = (
            rs_block(a, k, h, phase, q, 1) + got[OWN_R].astype(F32) + got[SUM_L].astype(F32)
        )

    def av_rows(h, phase, d, second=None):
        n = MANY // 32 if phase == 0 else MANY // 8
        start = h * (MANY // 2) + n * d
        if phase == 0:
            start = start + MANY // 8 * ring(h, 0)[0]
        if second is None:
            return pl.ds(pl.multiple_of(start, n), n)
        return pl.ds(pl.multiple_of(start + n // 2 * second, n // 2), n // 2)

    def av_move(a, k, h, phase, slot, where, device, send):
        ref = acts.at[a, k, where]
        sems = av_s.at[a, k, h, 4 * phase + slot], av_r.at[a, k, h, 4 * phase + slot]
        if send:
            push(ref, ref, *sems, device)
        else:
            arrived(ref, *sems, device)

    def av_first(a, k, h, phase):
        q, right, left = ring(h, 1 - phase)
        av_move(a, k, h, phase, 0, av_rows(h, phase, q), right, True)
        av_move(a, k, h, phase, 1, av_rows(h, phase, q), left, True)

    def far_parts(a, k, h, phase):
        if phase == 0:
            return (None, False) if (a + k + h) % 2 == 0 else (False, None)
        return 0, 1

    def av_second(a, k, h, phase):
        q, right, left = ring(h, 1 - phase)
        from_l, from_r = wrap(q - 1, RING), wrap(q + 1, RING)
        by_r, by_l = far_parts(a, k, h, phase)
        av_move(a, k, h, phase, 0, av_rows(h, phase, from_l), right, False)
        if by_r is not False:
            av_move(a, k, h, phase, 2, av_rows(h, phase, from_l, by_r), right, True)
        av_move(a, k, h, phase, 1, av_rows(h, phase, from_r), left, False)
        if by_l is not False:
            av_move(a, k, h, phase, 3, av_rows(h, phase, from_r, by_l), left, True)

    def av_last(a, k, h, phase):
        q, right, left = ring(h, 1 - phase)
        far = wrap(q + 2, RING)
        by_r, by_l = far_parts(a, k, h, phase)
        if by_r is not False:
            av_move(a, k, h, phase, 2, av_rows(h, phase, far, by_r), right, False)
        if by_l is not False:
            av_move(a, k, h, phase, 3, av_rows(h, phase, far, by_l), left, False)

    def own_rows(h):
        return av_rows(h, 0, ring(h, 1)[0])

    def hidden(k, h):
        gate = fin[0, k, h]
        acts[0, k, own_rows(h)] = (gate * jax.nn.sigmoid(gate) * fin[1, k, h]).astype(BF)
        av_first(0, k, h, 0)

    def act_grads(k, h):
        gate, upv, grad = fin[0, k, h], fin[1, k, h], fin[2, k, h]
        s = jax.nn.sigmoid(gate)
        acts[1, k, own_rows(h)] = (grad * upv * s * (1.0 + gate * (1.0 - s))).astype(BF)
        av_first(1, k, h, 0)
        acts[2, k, own_rows(h)] = (grad * (gate * s)).astype(BF)
        av_first(2, k, h, 0)

    def feature_part(b, a, k, c):
        cols = pl.ds(c * PIECE, PIECE)
        n = 256 // (2 * OWN)

        def body(i, where):
            if a == 0:
                tile = mm(acts[0, k, where], weight_d[:, cols], ((1,), (0,)))
            else:
                tile = mm(acts[a, k, where], weights[a - 1, cols, :], ((1,), (1,)))
            tile = tile.reshape(n, 2, OWN, PIECE)
            if a == 2:
                tile = tile + outs[b, k, c, pl.ds(n * i, n)]
            outs[b, k, c, pl.ds(n * i, n)] = tile

        tiles(body)
        if a != 1:
            push(outs.at[b, k, c, :, 1 - core], peer.at[b, k, c], ex_s.at[b, k, c], ex_r.at[b, k, c], other)

    def zr_move(b, k, c, way, n, send):
        where = pl.ds(0, OWN) if n < 4 else pl.ds(OWN // 2 * way, OWN // 2)
        sems = zr_s.at[b, k, c, way, n - 1], zr_r.at[b, k, c, way, n - 1]
        device = (up, down)[way]
        got = zgot.at[b, k, c, way, n - 1, where]
        if send:
            push(zsent.at[b, k, c, way, n - 1, where], got, *sems, device)
        else:
            arrived(got, *sems, device)

    def zr_step(b, k, c, n):
        if n == 4:
            arrived(peer.at[b, k, c], ex_s.at[b, k, c], ex_r.at[b, k, c], other)
        for way in range(2):
            target = wrap(z + n if way == 0 else z - n, DEPTH)
            if n == 4:
                where = pl.ds(OWN // 2 * way, OWN // 2)
                zsent[b, k, c, way, 3, where] = (
                    outs[b, k, c, target, core, where] + peer[b, k, c, target, where]
                )
            else:
                zr_move(b, k, c, way, n + 1, False)
                if n == 3:
                    fresh, rest = pl.ds(OWN // 2 * way, OWN // 2), pl.ds(OWN // 2 * (1 - way), OWN // 2)
                    zsent[b, k, c, way, 2, rest] = (
                        outs[b, k, c, target, core, rest] + peer[b, k, c, target, rest]
                    )
                    zsent[b, k, c, way, 2, fresh] = (
                        outs[b, k, c, target, core, fresh] + peer[b, k, c, target, fresh]
                        + zgot[b, k, c, way, 3, fresh]
                    )
                else:
                    zsent[b, k, c, way, n - 1] = (
                        outs[b, k, c, target, core] + peer[b, k, c, target] + zgot[b, k, c, way, n]
                    )
            zr_move(b, k, c, way, n, True)

    def zr_last(b, k, c):
        zr_move(b, k, c, 0, 1, False)
        zr_move(b, k, c, 1, 1, False)
        total = outs[b, k, c, z, core] + peer[b, k, c, z] + zgot[b, k, c, 0, 0] + zgot[b, k, c, 1, 0]
        (o_out, gt_out)[b][pl.ds(OWN * k, OWN), pl.ds(c * PIECE, PIECE)] = total.astype(BF)

    def over_tokens(left, right_side):
        total = mm(left(0).T, right_side(0), ((1,), (0,)))
        for k in range(1, CHUNKS):
            total = total + mm(left(k).T, right_side(k), ((1,), (0,)))
        return total

    def masked_store(out, mask, total, row, flip):
        for r in range(total.shape[0] // SIDE):
            for j in range(total.shape[1] // SIDE):
                factor = keep(mask, j, row + r) if flip else keep(mask, row + r, j)
                out[pl.ds((row + r) * SIDE, SIDE), pl.ds(j * SIDE, SIDE)] = (
                    total[r * SIDE : (r + 1) * SIDE, j * SIDE : (j + 1) * SIDE] * factor
                ).astype(BF)

    def grad_weight(a, i):
        cols = pl.ds(256 * i, 256)
        total = over_tokens(lambda k: rows[0, k, :, cols], lambda k: acts[1 + a, k])
        masked_store((gg_out, gu_out)[a], (gmask, umask)[a], total, 2 * i, False)

    def grad_down(i):
        cols = pl.ds(256 * i, min(256, 896 - 256 * i))
        total = over_tokens(lambda k: acts[0, k, :, cols], lambda k: rows[1, k])
        masked_store(gd_out, dmask, total, 2 * i, True)

    steps = dict(
        G=gather_start, N=gather_step, E=gather_end, M=mask_weight, P=partial,
        F=rs_first, S=rs_second, L=rs_last, H=hidden, Q=act_grads,
        A=av_first, B=av_second, C=av_last, T=feature_part, Z=zr_step, Y=zr_last,
        W=grad_weight, D=grad_down,
    )
    for code, *indices in SCHEDULE:
        steps[code](*indices)
    for copy in sends:
        copy.wait_send()


def store_kernel(*refs):
    sems = refs[-1]
    copies = [pltpu.make_async_copy(refs[i], refs[5 + i], sems.at[i]) for i in range(5)]
    for copy in copies:
        copy.start()
    for copy in copies:
        copy.wait()


def shards(tokens, grad_output, gate_weight, up_weight, down_weight, gate_mask, up_mask, down_mask):
    anywhere = pl.BlockSpec(memory_space=pl.ANY)
    vmem = pl.BlockSpec(memory_space=pltpu.VMEM)
    dma = pltpu.SemaphoreType.DMA
    d1, d2 = PHASE_DTYPES
    n = CHUNKS
    pieces = 512 // PIECE
    shapes = [(64, 512), (64, 512), (512, 896), (512, 896), (896, 512)]
    results = pl.pallas_call(
        kernel,
        out_shape=[pltpu.VMEM(shape, BF) for shape in shapes],
        in_specs=[anywhere] * 8,
        out_specs=[vmem] * 5,
        scratch_shapes=[
            pltpu.VMEM((2, n, MANY, 512), BF),
            pltpu.VMEM((2, 512, 896), BF),
            pltpu.VMEM((896, 512), BF),
            pltpu.VMEM((3, n, MANY, 896), F32),
            pltpu.VMEM((3, n, 2, 6, MANY // 16, 896), d1),
            pltpu.VMEM((3, n, 2, 6, MANY // 16, 896), d1),
            pltpu.VMEM((3, n, 2, MANY // 8, 896), F32),
            pltpu.VMEM((3, n, 2, 6, MANY // 64, 896), d2),
            pltpu.VMEM((3, n, 2, 6, MANY // 64, 896), d2),
            pltpu.VMEM((3, n, 2, MANY // 32, 896), F32),
            pltpu.VMEM((3, n, MANY, 896), BF),
            pltpu.VMEM((2, n, pieces, 8, 2, OWN, PIECE), F32),
            pltpu.VMEM((2, n, pieces, 8, OWN, PIECE), F32),
            pltpu.VMEM((2, n, pieces, 2, 4, OWN, PIECE), F32),
            pltpu.VMEM((2, n, pieces, 2, 4, OWN, PIECE), F32),
            pltpu.SMEM((4, 7), jnp.int32),
            pltpu.SMEM((4, 7), jnp.int32),
            pltpu.SMEM((4, 7), jnp.int32),
            dma((2, n, 16)), dma((2, n, 16)),
            dma((3, n, 2, 12)), dma((3, n, 2, 12)),
            dma((3, n, 2, 8)), dma((3, n, 2, 8)),
            dma((2, n, pieces)), dma((2, n, pieces)),
            dma((2, n, pieces, 2, 4)), dma((2, n, pieces, 2, 4)),
            dma((2 * n + 6,)),
        ],
        compiler_params=pltpu.CompilerParams(
            collective_id=0, has_side_effects=True, vmem_limit_bytes=58_000_000
        ),
        name="ffn",
    )(
        tokens, grad_output, gate_weight, up_weight, down_weight, gate_mask, up_mask, down_mask.T
    )
    return tuple(
        pl.pallas_call(
            store_kernel,
            out_shape=[jax.ShapeDtypeStruct(shape, BF) for shape in shapes],
            in_specs=[anywhere] * 5,
            out_specs=[anywhere] * 5,
            scratch_shapes=[dma((5,))],
            name="store",
        )(*[pltpu.with_memory_space_constraint(result, pltpu.VMEM) for result in results])
    )


def solution(mesh):
    return jax.shard_map(
        shards,
        mesh=mesh,
        in_specs=(
            P("tensor", "dp"),
            P("tensor", "dp"),
            P("dp", "tensor"),
            P("dp", "tensor"),
            P("tensor", "dp"),
            P("dp", "tensor"),
            P("dp", "tensor"),
            P("tensor", "dp"),
        ),
        out_specs=(
            P("tensor", "dp"),
            P("tensor", "dp"),
            P("dp", "tensor"),
            P("dp", "tensor"),
            P("tensor", "dp"),
        ),
        check_vma=False,
    )
```

time: 555 us -> 116 us (0.21)
  waiting for transfers between devices: 483 us -> 0 us
  Pallas kernels: 0 us -> 115 us
  matrix products: 31 us -> 0 us
  local copies, waits for them, and re-layouts: 15.3 us -> 0 us
  between operations: 14.3 us -> 0.8 us
  other arithmetic: 10.1 us -> 0 us
    reduce_scatter x3 -> x0, waiting for transfers between devices: 190 us -> none  [the longest x1 85.4 us: shards(): lax.psum_scatter(part_hidden, 'dp', scatter_dimension=0, tiled=True)]
    all_gather x4 -> x0, waiting for transfers between devices: 159 us -> none  [the longest x1 48 us: shards(): lax.all_gather(grad_up_act, 'dp', axis=0, tiled=True)]
    psum x1 -> x0, waiting for transfers between devices: 132 us -> none  [shards(): gate_full, up_full = lax.psum((part_gate, part_up), 'dp')]
    pallas_call x0 -> x2, Pallas kernels: none -> 115 us  [the longest x1 113 us: shards(): pl.pallas_call(kernel, out_shape=[pltpu.VMEM(shape, BF) for shape in shap...]
    dot_general x9 -> x0, matrix products: 31 us -> none  [the longest x3 12.9 us: contract_cols(): lax.dot_general(left, right_side, (((1,), (1,)), ((), ())), preferred_ele...]
    unnamed x31 -> x0, local copies, waits for them, and re-layouts: 13.7 us -> none
    convert_element_type x7 -> x0, other arithmetic: 10 us -> none  [the longest x1 4.26 us: shards(): (gate_full * jax.nn.sigmoid(gate_full) * up_full).astype(jnp.bfloat16)]
  transfers between devices with their start and end apart: 8 -> 0, of which waited for: 8 -> 0; matrix products, arithmetic and copies ran while one was open for 9% -> 0% of each run, Pallas kernels for 0% -> 0%
where the time goes in v2:
time: 116 us
  Pallas kernels  115 us (99%)
    pallas_call x1, Pallas kernels, shards(): pl.pallas_call(kernel, out_shape=[pltpu.VMEM(shape, BF) for shape in shap...  113 us

profile of v2, /device:TPU:8, one launch (start us, length us, event | category | flops | bytes accessed | tf_op | source)
XLA Modules:
  0.0 115.6 jit_solution(11518789101777719187)
XLA Ops:
  0.6 113.2 %ffn.1 = (bf16[64,512]{1,0:T(8,128)(2,1)S(1)}, bf16[64,512]{1,0:T(8,128)(2,1)S(1)}, bf16[512,896]{1,0:T(8,128)(2,1)S(1)}, bf16[512,896]{1,0:T(8,128)(2,1)S(1)}, bf16[896,512]{1,0:T(8,128)(2,1)S(1)}) custom-call(bf16[64,512]{1,0:T(8,128)(2,1)} %tok_in.1, bf16[64,512]{1,0:T(8,128)(2,1)} %cot_in.1, bf16[512,896]{1,0:T(8,128)(2,1)} %wg_in.1, ...), custom_call_target="tpu_custom_call" | custom-call | tf_op jit(solution)/shard_map/ffn/pallas_call | solution.py:659
  113.8 1.6 %store.1 = (bf16[64,512]{1,0:T(8,128)(2,1)}, bf16[64,512]{1,0:T(8,128)(2,1)}, bf16[512,896]{1,0:T(8,128)(2,1)}, bf16[512,896]{1,0:T(8,128)(2,1)}, bf16[896,512]{1,0:T(8,128)(2,1)}) custom-call(bf16[64,512]{1,0:T(8,128)(2,1)S(1)} %get-tuple-element.10.refs_0_, bf16[64,512]{1,0:T(8,128)(2,1)S(1)} %get-tuple-element.11.refs_1_, ...), custom_call_target="tpu_custom_call" | custom-call | tf_op jit(solution)/shard_map/store/pallas_call | solution.py:698

commit v3 on v2

v3 whole, which is shorter than its diff:
```python
import jax
import jax.numpy as jnp
from jax import lax
from jax.experimental import pallas as pl
from jax.experimental.pallas import tpu as pltpu
from jax.sharding import PartitionSpec as P

BF = jnp.bfloat16
F32 = jnp.float32
SIDE = 128
RING = 4
DEPTH = 8
CHUNKS = 2
OWN = 64 // CHUNKS
MANY = 1024 // CHUNKS
PIECE = 256
PHASE_DTYPES = (BF, F32)

SLOTS = (
    dict(FAR_R=0, FAR_L=1, OWN_R=2, OWN_L=3, SUM_R=4, SUM_L=5),
    dict(FAR_R=0, OWN_R=1, FAR_L=2, OWN_L=3, SUM_R=4, SUM_L=5),
)
SUMS = (pl.ds(0, 2), pl.ds(2, 1))
ACTS = (pl.ds(0, 1), pl.ds(1, 2))

SCHEDULE = (
    ("G", 0, 0),
    ("G", 1, 0),
    ("M", 0),
    ("M", 1),
    ("M", 2),
    ("N", 0, 0, 1),
    ("N", 0, 0, 7),
    ("N", 0, 0, 2),
    ("N", 0, 0, 6),
    ("N", 1, 0, 1),
    ("N", 1, 0, 2),
    ("N", 1, 0, 6),
    ("N", 1, 0, 7),
    ("G", 0, 1),
    ("N", 0, 0, 3),
    ("N", 0, 0, 5),
    ("N", 0, 0, 4),
    ("E", 0, 0),
    ("P", 0, 0),
    ("P", 1, 0),
    ("N", 1, 0, 4),
    ("F", 0, 0, 0, 0),
    ("F", 0, 0, 1, 0),
    ("N", 0, 1, 1),
    ("N", 0, 1, 2),
    ("N", 0, 1, 6),
    ("N", 0, 1, 7),
    ("G", 1, 1),
    ("N", 1, 0, 3),
    ("N", 1, 0, 5),
    ("E", 1, 0),
    ("P", 2, 0),
    ("F", 1, 0, 0, 0),
    ("F", 1, 0, 1, 0),
    ("S", 0, 0, 0, 0),
    ("S", 0, 0, 1, 0),
    ("N", 0, 1, 3),
    ("N", 0, 1, 4),
    ("N", 0, 1, 5),
    ("N", 1, 1, 1),
    ("N", 1, 1, 2),
    ("N", 1, 1, 7),
    ("N", 1, 1, 6),
    ("E", 0, 1),
    ("P", 0, 1),
    ("P", 1, 1),
    ("F", 0, 1, 0, 0),
    ("F", 0, 1, 1, 0),
    ("S", 1, 0, 0, 0),
    ("S", 1, 0, 1, 0),
    ("L", 0, 0, 0, 0),
    ("F", 0, 0, 0, 1),
    ("L", 0, 0, 1, 0),
    ("F", 0, 0, 1, 1),
    ("N", 1, 1, 3),
    ("N", 1, 1, 5),
    ("N", 1, 1, 4),
    ("S", 0, 1, 0, 0),
    ("E", 1, 1),
    ("P", 2, 1),
    ("F", 1, 1, 0, 0),
    ("F", 1, 1, 1, 0),
    ("S", 0, 1, 1, 0),
    ("L", 1, 0, 0, 0),
    ("F", 1, 0, 0, 1),
    ("L", 1, 0, 1, 0),
    ("F", 1, 0, 1, 1),
    ("S", 0, 0, 1, 1),
    ("S", 0, 0, 0, 1),
    ("S", 1, 1, 1, 0),
    ("L", 0, 1, 0, 0),
    ("F", 0, 1, 0, 1),
    ("S", 1, 1, 0, 0),
    ("L", 0, 1, 1, 0),
    ("F", 0, 1, 1, 1),
    ("S", 1, 0, 1, 1),
    ("S", 1, 0, 0, 1),
    ("L", 0, 0, 1, 1),
    ("H", 0, 1),
    ("L", 0, 0, 0, 1),
    ("H", 0, 0),
    ("L", 1, 1, 0, 0),
    ("F", 1, 1, 0, 1),
    ("L", 1, 1, 1, 0),
    ("F", 1, 1, 1, 1),
    ("S", 0, 1, 0, 1),
    ("S", 0, 1, 1, 1),
    ("L", 1, 0, 0, 1),
    ("Q", 0, 0),
    ("L", 1, 0, 1, 1),
    ("Q", 0, 1),
    ("B", 0, 0, 0, 0),
    ("B", 0, 0, 1, 0),
    ("S", 1, 1, 0, 1),
    ("S", 1, 1, 1, 1),
    ("L", 0, 1, 0, 1),
    ("H", 1, 0),
    ("L", 0, 1, 1, 1),
    ("H", 1, 1),
    ("B", 1, 0, 0, 0),
    ("B", 1, 0, 1, 0),
    ("C", 0, 0, 0, 0),
    ("A", 0, 0, 0, 1),
    ("C", 0, 0, 1, 0),
    ("A", 0, 0, 1, 1),
    ("L", 1, 1, 0, 1),
    ("Q", 1, 0),
    ("L", 1, 1, 1, 1),
    ("Q", 1, 1),
    ("B", 0, 1, 0, 0),
    ("B", 0, 1, 1, 0),
    ("C", 1, 0, 0, 0),
    ("A", 1, 0, 0, 1),
    ("C", 1, 0, 1, 0),
    ("A", 1, 0, 1, 1),
    ("B", 0, 0, 1, 1),
    ("B", 0, 0, 0, 1),
    ("B", 1, 1, 0, 0),
    ("B", 1, 1, 1, 0),
    ("C", 0, 1, 0, 0),
    ("A", 0, 1, 0, 1),
    ("C", 0, 1, 1, 0),
    ("A", 0, 1, 1, 1),
    ("B", 1, 0, 1, 1),
    ("B", 1, 0, 0, 1),
    ("C", 0, 0, 1, 1),
    ("C", 0, 0, 0, 1),
    ("T", 0, 0, 0, 0),
    ("T", 0, 0, 0, 1),
    ("C", 1, 1, 0, 0),
    ("C", 1, 1, 1, 0),
    ("A", 1, 1, 0, 1),
    ("A", 1, 1, 1, 1),
    ("Z", 0, 0, 0, 4),
    ("B", 0, 1, 0, 1),
    ("B", 0, 1, 1, 1),
    ("Z", 0, 0, 1, 4),
    ("C", 1, 0, 0, 1),
    ("C", 1, 0, 1, 1),
    ("T", 1, 1, 0, 0),
    ("T", 1, 1, 0, 1),
    ("T", 1, 2, 0, 0),
    ("T", 1, 2, 0, 1),
    ("Z", 0, 0, 0, 3),
    ("Z", 0, 0, 1, 3),
    ("Z", 1, 0, 0, 4),
    ("Z", 1, 0, 1, 4),
    ("B", 1, 1, 0, 1),
    ("B", 1, 1, 1, 1),
    ("Z", 0, 0, 0, 2),
    ("C", 0, 1, 0, 1),
    ("C", 0, 1, 1, 1),
    ("D", 2),
    ("Z", 0, 0, 1, 2),
    ("T", 0, 0, 1, 1),
    ("Z", 1, 0, 0, 3),
    ("D", 0),
    ("D", 1),
    ("Z", 1, 0, 1, 3),
    ("D", 3),
    ("T", 0, 0, 1, 0),
    ("Z", 0, 1, 1, 4),
    ("Z", 0, 0, 0, 1),
    ("C", 1, 1, 0, 1),
    ("Z", 0, 0, 1, 1),
    ("C", 1, 1, 1, 1),
    ("T", 1, 1, 1, 0),
    ("T", 1, 2, 1, 0),
    ("Z", 0, 1, 0, 4),
    ("Z", 1, 0, 0, 2),
    ("T", 1, 1, 1, 1),
    ("T", 1, 2, 1, 1),
    ("Z", 1, 0, 1, 2),
    ("W", 0, 0),
    ("Z", 0, 1, 1, 3),
    ("W", 1, 0),
    ("Y", 0, 0, 0),
    ("Z", 1, 1, 0, 4),
    ("W", 1, 1),
    ("W", 0, 1),
    ("Y", 0, 0, 1),
    ("Z", 1, 1, 1, 4),
    ("Z", 0, 1, 0, 3),
    ("Z", 1, 0, 0, 1),
    ("Z", 1, 0, 1, 1),
    ("Z", 0, 1, 1, 2),
    ("Z", 1, 1, 0, 3),
    ("Z", 1, 1, 1, 3),
    ("Z", 0, 1, 0, 2),
    ("Y", 1, 0, 0),
    ("Y", 1, 0, 1),
    ("Z", 0, 1, 1, 1),
    ("Z", 1, 1, 0, 2),
    ("Z", 1, 1, 1, 2),
    ("Z", 0, 1, 0, 1),
    ("Y", 0, 1, 1),
    ("Z", 1, 1, 0, 1),
    ("Z", 1, 1, 1, 1),
    ("Y", 0, 1, 0),
    ("Y", 1, 1, 0),
    ("Y", 1, 1, 1),
)


def mm(left, right_side, dims):
    return lax.dot_general(left, right_side, (dims, ((), ())), preferred_element_type=F32)


def kernel(
    tok_in, cot_in, wg_in, wu_in, wd_in, gm_in, um_in, dm_in,
    o_out, gt_out, gg_out, gu_out, gd_out,
    rows, weights, weight_d, part, sent1, got1, acc1, sent2, got2, fin,
    acts, outs, peer, zsent, zgot, gmask, umask, dmask,
    z_s, ag_r, rs_s, rs_r, av_s, av_r, ex_s, ex_r, zr_s, zr_r, loc,
):
    dp = lax.axis_index("dp")
    tensor = lax.axis_index("tensor")
    x, y = dp // RING, dp % RING
    z, core = tensor // 2, tensor % 2

    def wrap(value, n):
        return lax.rem(value + 2 * n, n)

    def at(dx=0, dy=0, dz=0, dc=0):
        return {
            "dp": wrap(x + dx, RING) * RING + wrap(y + dy, RING),
            "tensor": wrap(z + dz, DEPTH) * 2 + (1 - core if dc else core),
        }

    def remote(src, dst, s_sem, r_sem, device):
        return pltpu.make_async_remote_copy(
            src_ref=src, dst_ref=dst, send_sem=s_sem, recv_sem=r_sem,
            device_id=device, device_id_type=pl.DeviceIdType.MESH,
        )

    def push(src, dst, s_sem, r_sem, device):
        remote(src, dst, s_sem, r_sem, device).start()

    def arrived(dst, s_sem, r_sem):
        remote(dst, dst, s_sem, r_sem, at(dz=1)).wait_recv()

    def sent_all(src, s_sem):
        remote(src, src, s_sem, ex_r.at[0, 0, 0], at(dz=1)).wait_send()

    def block(i, k, zz, cc):
        return rows.at[i, k, wrap(zz, DEPTH), cc]

    row_loads = [
        [
            pltpu.make_async_copy(
                ref.at[pl.ds(OWN * k, OWN)], block(i, k, z, core), loc.at[CHUNKS * i + k]
            )
            for k in range(CHUNKS)
        ]
        for i, ref in enumerate((tok_in, cot_in))
    ]
    other_loads = [
        pltpu.make_async_copy(src, dst, loc.at[2 * CHUNKS + n])
        for n, (src, dst) in enumerate(
            (
                (gm_in, gmask), (um_in, umask), (dm_in, dmask),
                (wg_in, weights.at[0]), (wu_in, weights.at[1]), (wd_in, weight_d),
            )
        )
    ]
    for load in row_loads[0] + row_loads[1] + other_loads:
        load.start()

    barrier = pltpu.get_barrier_semaphore()
    peers = [at(dx=1), at(dx=-1), at(dy=1), at(dy=-1), at(dc=1)]
    peers += [at(dz=d) for d in (1, -1, 2, -2)]
    for device in peers:
        pl.semaphore_signal(barrier, inc=1, device_id=device, device_id_type=pl.DeviceIdType.MESH)
    pl.semaphore_wait(barrier, len(peers))

    up, down, other = at(dz=1), at(dz=-1), at(dc=1)

    def z_push(i, k, slot, ref, device):
        push(ref, ref, z_s.at[0], ag_r.at[i, k, slot], device)

    def z_share(i, k, zz):
        ref = block(i, k, zz, core)
        push(ref, ref, z_s.at[1], ag_r.at[i, k, 0], other)

    def z_arrived(i, k, slot, ref):
        arrived(ref, z_s.at[0], ag_r.at[i, k, slot])

    def gather_start(i, k):
        row_loads[i][k].wait()
        z_share(i, k, z)
        for d in (2, -2, 1, -1):
            z_push(i, k, d % DEPTH, block(i, k, z, core), at(dz=d))

    def gather_step(i, k, d):
        n = d if d < 4 else d - DEPTH
        ref = block(i, k, z - n, core)
        z_arrived(i, k, d, ref)
        if abs(n) == 1:
            z_push(i, k, 3 * n % DEPTH, ref, at(dz=2 * n))
        elif abs(n) == 2:
            z_push(i, k, 4, ref.at[pl.ds(0 if n > 0 else OWN // 2, OWN // 2)], at(dz=n))
        z_share(i, k, z - n)

    def gather_end(i, k):
        arrived(rows.at[i, k, :, 1 - core], z_s.at[1], ag_r.at[i, k, 0])

    def keep(mask, i, j):
        return mask[i, j].astype(F32)

    def mask_weight(n):
        for load in (other_loads[n], other_loads[3 + n]):
            load.wait()
        ref = weight_d if n == 2 else weights.at[n]
        n_rows, n_cols = (7, 4) if n == 2 else (4, 7)

        def body(i, carry):
            rows_i = pl.ds(pl.multiple_of(i * SIDE, SIDE), SIDE)
            for j in range(n_cols):
                cols = pl.ds(j * SIDE, SIDE)
                factor = keep(dmask, j, i) if n == 2 else keep((gmask, umask)[n], i, j)
                ref[rows_i, cols] = (ref[rows_i, cols].astype(F32) * factor).astype(BF)
            return carry

        lax.fori_loop(0, n_rows, body, 0)

    def tiles(body):
        def step(i, carry):
            body(i, pl.ds(pl.multiple_of(i * 256, 256), 256))
            return carry

        lax.fori_loop(0, MANY // 256, step, 0)

    def tile_rows(j, k, i):
        n = 256 // (2 * OWN)
        return rows[j, k, pl.ds(n * i, n)].reshape(256, 512)

    def partial(a, k):
        def body(i, where):
            if a < 2:
                part[a, k, where] = mm(tile_rows(0, k, i), weights[a], ((1,), (0,)))
            else:
                part[2, k, where] = mm(tile_rows(1, k, i), weight_d[...], ((1,), (1,)))

        tiles(body)

    def ring(h, phase):
        if (h + phase) % 2 == 0:
            return x, at(dx=1), at(dx=-1)
        return y, at(dy=1), at(dy=-1)

    def rs_refs(u, k, h, phase):
        which = SUMS[u]
        if phase == 0:
            return (
                part.at[which, k], h * (MANY // 2), MANY // 16,
                sent1.at[which, k, h], got1.at[which, k, h], acc1.at[which, k, h],
            )
        return (
            acc1.at[which, k, h], 0, MANY // 64,
            sent2.at[which, k, h], got2.at[which, k, h], fin.at[which, k, h],
        )

    def rs_sems(u, k, h, phase, n):
        return rs_s.at[phase], rs_r.at[u, k, h, 3 * phase + n]

    def rs_push(u, k, h, phase, first, count, n, device):
        _, _, _, sent, got, _ = rs_refs(u, k, h, phase)
        where = pl.ds(first, count)
        push(sent.at[:, where], got.at[:, where], *rs_sems(u, k, h, phase, n), device)

    def rs_arrived(u, k, h, phase, first, count, n):
        got = rs_refs(u, k, h, phase)[4]
        arrived(got.at[:, pl.ds(first, count)], *rs_sems(u, k, h, phase, n))

    def rs_block(u, k, h, phase, d, second):
        src, base, n, _, _, _ = rs_refs(u, k, h, phase)
        start = base + 2 * n * d + n * second
        return src[:, pl.ds(pl.multiple_of(start, n), n), :]

    def rs_first(u, k, h, phase):
        q, right, left = ring(h, phase)
        sent = rs_refs(u, k, h, phase)[3]
        dtype = PHASE_DTYPES[phase]
        slots = SLOTS[phase]
        far, to_r, to_l = wrap(q + 2, RING), wrap(q + 1, RING), wrap(q - 1, RING)
        plan = (
            ("FAR_R", far, 0, right, 0), ("FAR_L", far, 1, left, 1),
            ("OWN_R", to_r, 1, right, 2), ("OWN_L", to_l, 0, left, 2),
        )
        for name, d, second, device, n in plan:
            sent[:, slots[name]] = rs_block(u, k, h, phase, d, second).astype(dtype)
            if phase == 0:
                rs_push(u, k, h, 0, slots[name], 1, n, device)
            elif n == 2:
                rs_push(u, k, h, 1, slots[name] - 1, 2, 0 if device is right else 1, device)

    def rs_second(u, k, h, phase):
        q, right, left = ring(h, phase)
        _, _, _, sent, got, _ = rs_refs(u, k, h, phase)
        dtype = PHASE_DTYPES[phase]
        slots = SLOTS[phase]
        for way, d, second, device, n in (
            ("_R", wrap(q + 1, RING), 0, right, 0), ("_L", wrap(q - 1, RING), 1, left, 1),
        ):
            far, out = slots["FAR" + way], slots["SUM" + way]
            rs_arrived(u, k, h, phase, far, 1 + phase, n)
            sent[:, out] = (rs_block(u, k, h, phase, d, second) + got[:, far].astype(F32)).astype(dtype)
            rs_push(u, k, h, phase, out, 1, 2, device)

    def rs_last(u, k, h, phase):
        q = ring(h, phase)[0]
        _, _, n, _, got, dst = rs_refs(u, k, h, phase)
        slots = SLOTS[phase]
        rs_arrived(u, k, h, phase, 2 + 2 * phase, 4 - 2 * phase, 2)
        for second, one, two in ((0, "SUM_R", "OWN_L"), (1, "OWN_R", "SUM_L")):
            dst[:, pl.ds(n * second, n), :] = (
                rs_block(u, k, h, phase, q, second)
                + got[:, slots[one]].astype(F32) + got[:, slots[two]].astype(F32)
            )

    def av_rows(h, phase, d, second=None):
        n = MANY // 32 if phase == 0 else MANY // 8
        start = h * (MANY // 2) + n * d
        if phase == 0:
            start = start + MANY // 8 * ring(h, 0)[0]
        if second is None:
            return pl.ds(pl.multiple_of(start, n), n)
        return pl.ds(pl.multiple_of(start + n // 2 * second, n // 2), n // 2)

    def av_move(v, k, h, phase, slot, where, device=None):
        ref = acts.at[ACTS[v], k, where]
        sems = av_s.at[0], av_r.at[v, k, h, 3 * phase + slot]
        if device is None:
            arrived(ref, *sems)
        else:
            push(ref, ref, *sems, device)

    def av_first(v, k, h, phase):
        q, right, left = ring(h, 1 - phase)
        av_move(v, k, h, phase, 0, av_rows(h, phase, q), right)
        av_move(v, k, h, phase, 1, av_rows(h, phase, q), left)

    def av_second(v, k, h, phase):
        q, right, left = ring(h, 1 - phase)
        for slot, d, device, part_of in (
            (0, wrap(q - 1, RING), right, 0), (1, wrap(q + 1, RING), left, 1),
        ):
            av_move(v, k, h, phase, slot, av_rows(h, phase, d))
            if phase == 1:
                av_move(v, k, h, 1, 2, av_rows(h, 1, d, part_of), device)
            elif (v + k + h) % 2 == slot:
                av_move(v, k, h, 0, 2, av_rows(h, 0, d), device)

    def av_last(v, k, h, phase):
        q = ring(h, 1 - phase)[0]
        av_move(v, k, h, phase, 2, av_rows(h, phase, wrap(q + 2, RING)))

    def own_rows(h):
        return av_rows(h, 0, ring(h, 1)[0])

    def hidden(k, h):
        gate = fin[0, k, h]
        acts[0, k, own_rows(h)] = (gate * jax.nn.sigmoid(gate) * fin[1, k, h]).astype(BF)
        av_first(0, k, h, 0)

    def act_grads(k, h):
        gate, upv, grad = fin[0, k, h], fin[1, k, h], fin[2, k, h]
        s = jax.nn.sigmoid(gate)
        acts[1, k, own_rows(h)] = (grad * upv * s * (1.0 + gate * (1.0 - s))).astype(BF)
        acts[2, k, own_rows(h)] = (grad * (gate * s)).astype(BF)
        av_first(1, k, h, 0)

    def feature_part(b, a, k, c):
        cols = pl.ds(c * PIECE, PIECE)
        n = 256 // (2 * OWN)

        def body(i, where):
            if a == 0:
                tile = mm(acts[0, k, where], weight_d[:, cols], ((1,), (0,)))
            else:
                tile = mm(acts[a, k, where], weights[a - 1, cols, :], ((1,), (1,)))
            tile = tile.reshape(n, 2, OWN, PIECE)
            if a == 2:
                tile = tile + outs[b, k, c, pl.ds(n * i, n)]
            outs[b, k, c, pl.ds(n * i, n)] = tile

        tiles(body)
        if a != 1:
            push(outs.at[b, k, c, :, 1 - core], peer.at[b, k, c], ex_s.at[0], ex_r.at[b, k, c], other)

    def zr_move(b, k, c, way, n, send):
        where = pl.ds(0, OWN) if n < 4 else pl.ds(OWN // 2 * way, OWN // 2)
        sems = zr_s.at[n // 4], zr_r.at[b, k, c, 3 * way + n - 2 if n > 1 else 6]
        got = zgot.at[b, k, c, way, n - 1, where]
        if send:
            push(zsent.at[b, k, c, way, n - 1, where], got, *sems, (up, down)[way])
        else:
            arrived(got, *sems)

    def zr_step(b, k, c, n):
        if n == 4:
            arrived(peer.at[b, k, c], ex_s.at[0], ex_r.at[b, k, c])
        for way in range(2):
            target = wrap(z + n if way == 0 else z - n, DEPTH)
            if n == 4:
                where = pl.ds(OWN // 2 * way, OWN // 2)
                zsent[b, k, c, way, 3, where] = (
                    outs[b, k, c, target, core, where] + peer[b, k, c, target, where]
                )
            else:
                zr_move(b, k, c, way, n + 1, False)
                if n == 3:
                    fresh, rest = pl.ds(OWN // 2 * way, OWN // 2), pl.ds(OWN // 2 * (1 - way), OWN // 2)
                    zsent[b, k, c, way, 2, rest] = (
                        outs[b, k, c, target, core, rest] + peer[b, k, c, target, rest]
                    )
                    zsent[b, k, c, way, 2, fresh] = (
                        outs[b, k, c, target, core, fresh] + peer[b, k, c, target, fresh]
                        + zgot[b, k, c, way, 3, fresh]
                    )
                else:
                    zsent[b, k, c, way, n - 1] = (
                        outs[b, k, c, target, core] + peer[b, k, c, target] + zgot[b, k, c, way, n]
                    )
            zr_move(b, k, c, way, n, True)

    def zr_last(b, k, c):
        arrived(zgot.at[b, k, c, :, 0], zr_s.at[0], zr_r.at[b, k, c, 6])
        total = outs[b, k, c, z, core] + peer[b, k, c, z] + zgot[b, k, c, 0, 0] + zgot[b, k, c, 1, 0]
        (o_out, gt_out)[b][pl.ds(OWN * k, OWN), pl.ds(c * PIECE, PIECE)] = total.astype(BF)

    def over_tokens(left, right_side):
        total = mm(left(0).T, right_side(0), ((1,), (0,)))
        for k in range(1, CHUNKS):
            total = total + mm(left(k).T, right_side(k), ((1,), (0,)))
        return total

    def masked_store(out, mask, total, row, flip):
        for r in range(total.shape[0] // SIDE):
            for j in range(total.shape[1] // SIDE):
                factor = keep(mask, j, row + r) if flip else keep(mask, row + r, j)
                out[pl.ds((row + r) * SIDE, SIDE), pl.ds(j * SIDE, SIDE)] = (
                    total[r * SIDE : (r + 1) * SIDE, j * SIDE : (j + 1) * SIDE] * factor
                ).astype(BF)

    def grad_weight(a, i):
        cols = pl.ds(256 * i, 256)
        total = over_tokens(lambda k: rows[0, k, :, :, :, cols].reshape(MANY, 256), lambda k: acts[1 + a, k])
        masked_store((gg_out, gu_out)[a], (gmask, umask)[a], total, 2 * i, False)

    def grad_down(i):
        cols = pl.ds(256 * i, min(256, 896 - 256 * i))
        total = over_tokens(lambda k: acts[0, k, :, cols], lambda k: rows[1, k].reshape(MANY, 512))
        masked_store(gd_out, dmask, total, 2 * i, True)

    steps = dict(
        G=gather_start, N=gather_step, E=gather_end, M=mask_weight, P=partial,
        F=rs_first, S=rs_second, L=rs_last, H=hidden, Q=act_grads,
        A=av_first, B=av_second, C=av_last, T=feature_part, Z=zr_step, Y=zr_last,
        W=grad_weight, D=grad_down,
    )
    for code, *indices in SCHEDULE:
        steps[code](*indices)
    sent_all(rows.at[:, :, pl.ds(0, DEPTH - 1), 0], z_s.at[0])
    sent_all(rows.at[:, :, :, 0], z_s.at[1])
    sent_all(sent1, rs_s.at[0])
    sent_all(sent2, rs_s.at[1])
    sent_all(acts.at[:, :, pl.ds(0, MANY // 16 * 15)], av_s.at[0])
    sent_all(peer, ex_s.at[0])
    sent_all(zsent.at[:, :, :, :, pl.ds(0, 3)], zr_s.at[0])
    sent_all(zsent.at[:, :, :, :, 3, pl.ds(0, OWN // 2)], zr_s.at[1])


def store_kernel(*refs):
    sems = refs[-1]
    copies = [pltpu.make_async_copy(refs[i], refs[5 + i], sems.at[i]) for i in range(5)]
    for copy in copies:
        copy.start()
    for copy in copies:
        copy.wait()


def shards(tokens, grad_output, gate_weight, up_weight, down_weight, gate_mask, up_mask, down_mask):
    anywhere = pl.BlockSpec(memory_space=pl.ANY)
    vmem = pl.BlockSpec(memory_space=pltpu.VMEM)
    dma = pltpu.SemaphoreType.DMA
    d1, d2 = PHASE_DTYPES
    n = CHUNKS
    pieces = 512 // PIECE
    shapes = [(64, 512), (64, 512), (512, 896), (512, 896), (896, 512)]
    results = pl.pallas_call(
        kernel,
        out_shape=[pltpu.VMEM(shape, BF) for shape in shapes],
        in_specs=[anywhere] * 8,
        out_specs=[vmem] * 5,
        scratch_shapes=[
            pltpu.VMEM((2, n, DEPTH, 2, OWN, 512), BF),
            pltpu.VMEM((2, 512, 896), BF),
            pltpu.VMEM((896, 512), BF),
            pltpu.VMEM((3, n, MANY, 896), F32),
            pltpu.VMEM((3, n, 2, 6, MANY // 16, 896), d1),
            pltpu.VMEM((3, n, 2, 6, MANY // 16, 896), d1),
            pltpu.VMEM((3, n, 2, MANY // 8, 896), F32),
            pltpu.VMEM((3, n, 2, 6, MANY // 64, 896), d2),
            pltpu.VMEM((3, n, 2, 6, MANY // 64, 896), d2),
            pltpu.VMEM((3, n, 2, MANY // 32, 896), F32),
            pltpu.VMEM((3, n, MANY, 896), BF),
            pltpu.VMEM((2, n, pieces, 8, 2, OWN, PIECE), F32),
            pltpu.VMEM((2, n, pieces, 8, OWN, PIECE), F32),
            pltpu.VMEM((2, n, pieces, 2, 4, OWN, PIECE), F32),
            pltpu.VMEM((2, n, pieces, 2, 4, OWN, PIECE), F32),
            pltpu.SMEM((4, 7), jnp.int32),
            pltpu.SMEM((4, 7), jnp.int32),
            pltpu.SMEM((4, 7), jnp.int32),
            dma((2,)), dma((2, n, 8)),
            dma((2,)), dma((2, n, 2, 6)),
            dma((1,)), dma((2, n, 2, 6)),
            dma((1,)), dma((2, n, pieces)),
            dma((2,)), dma((2, n, pieces, 7)),
            dma((2 * n + 6,)),
        ],
        compiler_params=pltpu.CompilerParams(
            collective_id=0, has_side_effects=True, vmem_limit_bytes=58_000_000
        ),
        name="ffn",
    )(
        tokens, grad_output, gate_weight, up_weight, down_weight, gate_mask, up_mask, down_mask.T
    )
    return tuple(
        pl.pallas_call(
            store_kernel,
            out_shape=[jax.ShapeDtypeStruct(shape, BF) for shape in shapes],
            in_specs=[anywhere] * 5,
            out_specs=[anywhere] * 5,
            scratch_shapes=[dma((5,))],
            name="store",
        )(*[pltpu.with_memory_space_constraint(result, pltpu.VMEM) for result in results])
    )


def solution(mesh):
    return jax.shard_map(
        shards,
        mesh=mesh,
        in_specs=(
            P("tensor", "dp"),
            P("tensor", "dp"),
            P("dp", "tensor"),
            P("dp", "tensor"),
            P("tensor", "dp"),
            P("dp", "tensor"),
            P("dp", "tensor"),
            P("tensor", "dp"),
        ),
        out_specs=(
            P("tensor", "dp"),
            P("tensor", "dp"),
            P("dp", "tensor"),
            P("dp", "tensor"),
            P("tensor", "dp"),
        ),
        check_vma=False,
    )
```

time: 116 us -> 112 us (0.966)
  Pallas kernels: 115 us -> 111 us
    pallas_call x1, Pallas kernels: 113 us -> 110 us  [shards(): pl.pallas_call(kernel, out_shape=[pltpu.VMEM(shape, BF) for shape in shap...]
where the time goes in v3:
time: 112 us
  Pallas kernels  111 us (99%)
    pallas_call x1, Pallas kernels, shards(): pl.pallas_call(kernel, out_shape=[pltpu.VMEM(shape, BF) for shape in shap...  110 us

profile of v3, /device:TPU:8, one launch (start us, length us, event | category | flops | bytes accessed | tf_op | source)
XLA Modules:
  0.0 112.1 jit_solution(16294510431031973827)
XLA Ops:
  0.6 109.8 %ffn.1 = (bf16[64,512]{1,0:T(8,128)(2,1)S(1)}, bf16[64,512]{1,0:T(8,128)(2,1)S(1)}, bf16[512,896]{1,0:T(8,128)(2,1)S(1)}, bf16[512,896]{1,0:T(8,128)(2,1)S(1)}, bf16[896,512]{1,0:T(8,128)(2,1)S(1)}) custom-call(bf16[64,512]{1,0:T(8,128)(2,1)} %tok_in.1, bf16[64,512]{1,0:T(8,128)(2,1)} %cot_in.1, bf16[512,896]{1,0:T(8,128)(2,1)} %wg_in.1, ...), custom_call_target="tpu_custom_call" | custom-call | tf_op jit(solution)/shard_map/ffn/pallas_call | solution.py:617
  110.4 1.6 %store.1 = (bf16[64,512]{1,0:T(8,128)(2,1)}, bf16[64,512]{1,0:T(8,128)(2,1)}, bf16[512,896]{1,0:T(8,128)(2,1)}, bf16[512,896]{1,0:T(8,128)(2,1)}, bf16[896,512]{1,0:T(8,128)(2,1)}) custom-call(bf16[64,512]{1,0:T(8,128)(2,1)S(1)} %get-tuple-element.10.refs_0_, bf16[64,512]{1,0:T(8,128)(2,1)S(1)} %get-tuple-element.11.refs_1_, ...), custom_call_target="tpu_custom_call" | custom-call | tf_op jit(solution)/shard_map/store/pallas_call | solution.py:656

commit v4 on v3

--- a/solution.py
+++ b/solution.py
@@ -31,8 +31,8 @@
     ("M", 2),
     ("N", 0, 0, 1),
     ("N", 0, 0, 7),
+    ("N", 0, 0, 6),
     ("N", 0, 0, 2),
-    ("N", 0, 0, 6),
     ("N", 1, 0, 1),
     ("N", 1, 0, 2),
     ("N", 1, 0, 6),
@@ -42,18 +42,18 @@
     ("N", 0, 0, 5),
     ("N", 0, 0, 4),
     ("E", 0, 0),
+    ("P", 1, 0),
+    ("N", 1, 0, 3),
     ("P", 0, 0),
-    ("P", 1, 0),
     ("N", 1, 0, 4),
     ("F", 0, 0, 0, 0),
+    ("N", 1, 0, 5),
     ("F", 0, 0, 1, 0),
     ("N", 0, 1, 1),
     ("N", 0, 1, 2),
     ("N", 0, 1, 6),
     ("N", 0, 1, 7),
     ("G", 1, 1),
-    ("N", 1, 0, 3),
-    ("N", 1, 0, 5),
     ("E", 1, 0),
     ("P", 2, 0),
     ("F", 1, 0, 0, 0),
@@ -65,164 +65,164 @@
     ("N", 0, 1, 5),
     ("N", 1, 1, 1),
     ("N", 1, 1, 2),
+    ("E", 0, 1),
+    ("P", 1, 1),
+    ("N", 1, 1, 6),
     ("N", 1, 1, 7),
-    ("N", 1, 1, 6),
-    ("E", 0, 1),
     ("P", 0, 1),
-    ("P", 1, 1),
+    ("S", 1, 0, 0, 0),
+    ("S", 1, 0, 1, 0),
     ("F", 0, 1, 0, 0),
     ("F", 0, 1, 1, 0),
-    ("S", 1, 0, 0, 0),
-    ("S", 1, 0, 1, 0),
     ("L", 0, 0, 0, 0),
     ("F", 0, 0, 0, 1),
     ("L", 0, 0, 1, 0),
     ("F", 0, 0, 1, 1),
     ("N", 1, 1, 3),
+    ("L", 1, 0, 0, 0),
+    ("N", 1, 1, 4),
+    ("F", 1, 0, 0, 1),
+    ("L", 1, 0, 1, 0),
+    ("F", 1, 0, 1, 1),
     ("N", 1, 1, 5),
-    ("N", 1, 1, 4),
-    ("S", 0, 1, 0, 0),
     ("E", 1, 1),
     ("P", 2, 1),
     ("F", 1, 1, 0, 0),
+    ("S", 0, 1, 1, 0),
+    ("S", 0, 1, 0, 0),
     ("F", 1, 1, 1, 0),
-    ("S", 0, 1, 1, 0),
-    ("L", 1, 0, 0, 0),
-    ("F", 1, 0, 0, 1),
-    ("L", 1, 0, 1, 0),
-    ("F", 1, 0, 1, 1),
     ("S", 0, 0, 1, 1),
     ("S", 0, 0, 0, 1),
+    ("S", 1, 0, 1, 1),
+    ("S", 1, 0, 0, 1),
+    ("S", 1, 1, 0, 0),
+    ("L", 0, 1, 1, 0),
+    ("F", 0, 1, 1, 1),
     ("S", 1, 1, 1, 0),
     ("L", 0, 1, 0, 0),
     ("F", 0, 1, 0, 1),
-    ("S", 1, 1, 0, 0),
-    ("L", 0, 1, 1, 0),
-    ("F", 0, 1, 1, 1),
-    ("S", 1, 0, 1, 1),
-    ("S", 1, 0, 0, 1),
     ("L", 0, 0, 1, 1),
     ("H", 0, 1),
     ("L", 0, 0, 0, 1),
     ("H", 0, 0),
+    ("L", 1, 0, 1, 1),
+    ("Q", 0, 1),
+    ("L", 1, 0, 0, 1),
+    ("Q", 0, 0),
     ("L", 1, 1, 0, 0),
     ("F", 1, 1, 0, 1),
     ("L", 1, 1, 1, 0),
     ("F", 1, 1, 1, 1),
+    ("S", 0, 1, 1, 1),
+    ("B", 0, 0, 1, 0),
     ("S", 0, 1, 0, 1),
-    ("S", 0, 1, 1, 1),
-    ("L", 1, 0, 0, 1),
-    ("Q", 0, 0),
-    ("L", 1, 0, 1, 1),
-    ("Q", 0, 1),
     ("B", 0, 0, 0, 0),
-    ("B", 0, 0, 1, 0),
+    ("B", 1, 0, 1, 0),
+    ("B", 1, 0, 0, 0),
+    ("S", 1, 1, 1, 1),
     ("S", 1, 1, 0, 1),
-    ("S", 1, 1, 1, 1),
+    ("L", 0, 1, 1, 1),
+    ("H", 1, 1),
+    ("C", 0, 0, 1, 0),
+    ("A", 0, 0, 1, 1),
     ("L", 0, 1, 0, 1),
     ("H", 1, 0),
-    ("L", 0, 1, 1, 1),
-    ("H", 1, 1),
-    ("B", 1, 0, 0, 0),
-    ("B", 1, 0, 1, 0),
     ("C", 0, 0, 0, 0),
     ("A", 0, 0, 0, 1),
-    ("C", 0, 0, 1, 0),
-    ("A", 0, 0, 1, 1),
+    ("C", 1, 0, 1, 0),
+    ("A", 1, 0, 1, 1),
+    ("L", 1, 1, 1, 1),
+    ("Q", 1, 1),
+    ("C", 1, 0, 0, 0),
+    ("A", 1, 0, 0, 1),
     ("L", 1, 1, 0, 1),
     ("Q", 1, 0),
-    ("L", 1, 1, 1, 1),
-    ("Q", 1, 1),
-    ("B", 0, 1, 0, 0),
     ("B", 0, 1, 1, 0),
-    ("C", 1, 0, 0, 0),
-    ("A", 1, 0, 0, 1),
-    ("C", 1, 0, 1, 0),
-    ("A", 1, 0, 1, 1),
     ("B", 0, 0, 1, 1),
     ("B", 0, 0, 0, 1),
+    ("B", 0, 1, 0, 0),
+    ("B", 1, 1, 1, 0),
+    ("B", 1, 0, 1, 1),
+    ("B", 1, 0, 0, 1),
     ("B", 1, 1, 0, 0),
-    ("B", 1, 1, 1, 0),
+    ("C", 0, 1, 1, 0),
+    ("A", 0, 1, 1, 1),
+    ("C", 0, 0, 1, 1),
     ("C", 0, 1, 0, 0),
     ("A", 0, 1, 0, 1),
-    ("C", 0, 1, 1, 0),
-    ("A", 0, 1, 1, 1),
-    ("B", 1, 0, 1, 1),
-    ("B", 1, 0, 0, 1),
-    ("C", 0, 0, 1, 1),
     ("C", 0, 0, 0, 1),
     ("T", 0, 0, 0, 0),
     ("T", 0, 0, 0, 1),
+    ("C", 1, 1, 1, 0),
+    ("A", 1, 1, 1, 1),
+    ("C", 1, 0, 1, 1),
+    ("Z", 0, 0, 0, 4),
     ("C", 1, 1, 0, 0),
-    ("C", 1, 1, 1, 0),
     ("A", 1, 1, 0, 1),
-    ("A", 1, 1, 1, 1),
-    ("Z", 0, 0, 0, 4),
-    ("B", 0, 1, 0, 1),
-    ("B", 0, 1, 1, 1),
-    ("Z", 0, 0, 1, 4),
     ("C", 1, 0, 0, 1),
-    ("C", 1, 0, 1, 1),
     ("T", 1, 1, 0, 0),
     ("T", 1, 1, 0, 1),
     ("T", 1, 2, 0, 0),
+    ("B", 0, 1, 1, 1),
     ("T", 1, 2, 0, 1),
+    ("B", 0, 1, 0, 1),
+    ("Z", 0, 0, 1, 4),
+    ("Z", 1, 0, 0, 4),
     ("Z", 0, 0, 0, 3),
+    ("Z", 1, 0, 1, 4),
+    ("B", 1, 1, 1, 1),
     ("Z", 0, 0, 1, 3),
-    ("Z", 1, 0, 0, 4),
-    ("Z", 1, 0, 1, 4),
     ("B", 1, 1, 0, 1),
-    ("B", 1, 1, 1, 1),
+    ("Z", 1, 0, 0, 3),
     ("Z", 0, 0, 0, 2),
+    ("Z", 1, 0, 1, 3),
+    ("C", 0, 1, 1, 1),
     ("C", 0, 1, 0, 1),
-    ("C", 0, 1, 1, 1),
-    ("D", 2),
+    ("T", 0, 0, 1, 0),
+    ("T", 0, 0, 1, 1),
     ("Z", 0, 0, 1, 2),
-    ("T", 0, 0, 1, 1),
-    ("Z", 1, 0, 0, 3),
     ("D", 0),
     ("D", 1),
-    ("Z", 1, 0, 1, 3),
-    ("D", 3),
-    ("T", 0, 0, 1, 0),
-    ("Z", 0, 1, 1, 4),
+    ("C", 1, 1, 1, 1),
+    ("Z", 1, 0, 0, 2),
+    ("D", 2),
     ("Z", 0, 0, 0, 1),
     ("C", 1, 1, 0, 1),
-    ("Z", 0, 0, 1, 1),
-    ("C", 1, 1, 1, 1),
     ("T", 1, 1, 1, 0),
+    ("T", 1, 1, 1, 1),
     ("T", 1, 2, 1, 0),
     ("Z", 0, 1, 0, 4),
-    ("Z", 1, 0, 0, 2),
-    ("T", 1, 1, 1, 1),
+    ("Z", 0, 1, 1, 4),
+    ("Z", 1, 0, 1, 2),
     ("T", 1, 2, 1, 1),
-    ("Z", 1, 0, 1, 2),
+    ("D", 3),
+    ("Z", 0, 0, 1, 1),
     ("W", 0, 0),
+    ("Z", 1, 1, 0, 4),
+    ("W", 0, 1),
+    ("Z", 1, 0, 0, 1),
+    ("W", 1, 0),
+    ("Z", 1, 1, 1, 4),
+    ("Y", 0, 0, 0),
+    ("W", 1, 1),
+    ("Z", 0, 1, 0, 3),
     ("Z", 0, 1, 1, 3),
-    ("W", 1, 0),
-    ("Y", 0, 0, 0),
-    ("Z", 1, 1, 0, 4),
-    ("W", 1, 1),
-    ("W", 0, 1),
+    ("Z", 1, 0, 1, 1),
     ("Y", 0, 0, 1),
-    ("Z", 1, 1, 1, 4),
-    ("Z", 0, 1, 0, 3),
-    ("Z", 1, 0, 0, 1),
-    ("Z", 1, 0, 1, 1),
-    ("Z", 0, 1, 1, 2),
     ("Z", 1, 1, 0, 3),
+    ("Y", 1, 0, 0),
     ("Z", 1, 1, 1, 3),
     ("Z", 0, 1, 0, 2),
-    ("Y", 1, 0, 0),
+    ("Z", 0, 1, 1, 2),
     ("Y", 1, 0, 1),
-    ("Z", 0, 1, 1, 1),
     ("Z", 1, 1, 0, 2),
     ("Z", 1, 1, 1, 2),
     ("Z", 0, 1, 0, 1),
-    ("Y", 0, 1, 1),
+    ("Z", 0, 1, 1, 1),
     ("Z", 1, 1, 0, 1),
     ("Z", 1, 1, 1, 1),
     ("Y", 0, 1, 0),
+    ("Y", 0, 1, 1),
     ("Y", 1, 1, 0),
     ("Y", 1, 1, 1),
 )
@@ -463,15 +463,19 @@
 
     def av_first(v, k, h, phase):
         q, right, left = ring(h, 1 - phase)
-        av_move(v, k, h, phase, 0, av_rows(h, phase, q), right)
-        av_move(v, k, h, phase, 1, av_rows(h, phase, q), left)
+        if phase == 0:
+            av_move(v, k, h, 0, 0, av_rows(h, 0, q), right)
+            av_move(v, k, h, 0, 1, av_rows(h, 0, q), left)
+            return
+        for slot, part_of, device in ((0, 0, right), (1, 1, left), (3, 1, right), (4, 0, left)):
+            av_move(v, k, h, 1, slot, av_rows(h, 1, q, part_of), device)
 
     def av_second(v, k, h, phase):
         q, right, left = ring(h, 1 - phase)
         for slot, d, device, part_of in (
             (0, wrap(q - 1, RING), right, 0), (1, wrap(q + 1, RING), left, 1),
         ):
-            av_move(v, k, h, phase, slot, av_rows(h, phase, d))
+            av_move(v, k, h, phase, slot, av_rows(h, phase, d, part_of if phase == 1 else None))
             if phase == 1:
                 av_move(v, k, h, 1, 2, av_rows(h, 1, d, part_of), device)
             elif (v + k + h) % 2 == slot:
@@ -479,6 +483,9 @@
 
     def av_last(v, k, h, phase):
         q = ring(h, 1 - phase)[0]
+        if phase == 1:
+            av_move(v, k, h, 1, 3, av_rows(h, 1, wrap(q - 1, RING), 1))
+            av_move(v, k, h, 1, 4, av_rows(h, 1, wrap(q + 1, RING), 0))
         av_move(v, k, h, phase, 2, av_rows(h, phase, wrap(q + 2, RING)))
 
     def own_rows(h):
@@ -640,7 +647,7 @@
             pltpu.SMEM((4, 7), jnp.int32),
             dma((2,)), dma((2, n, 8)),
             dma((2,)), dma((2, n, 2, 6)),
-            dma((1,)), dma((2, n, 2, 6)),
+            dma((1,)), dma((2, n, 2, 8)),
             dma((1,)), dma((2, n, pieces)),
             dma((2,)), dma((2, n, pieces, 7)),
             dma((2 * n + 6,)),

time: 112 us -> 110 us (0.982)
  Pallas kernels: 111 us -> 109 us
    pallas_call x1, Pallas kernels: 110 us -> 107 us  [shards(): pl.pallas_call(kernel, out_shape=[pltpu.VMEM(shape, BF) for shape in shap...]
where the time goes in v4:
time: 110 us; the launch traced here: 109 us
  Pallas kernels  109 us (99%)
    pallas_call x1, Pallas kernels, shards(): pl.pallas_call(kernel, out_shape=[pltpu.VMEM(shape, BF) for shape in shap...  107 us

profile of v4, /device:TPU:8, one launch (start us, length us, event | category | flops | bytes accessed | tf_op | source)
XLA Modules:
  0.0 109.2 jit_solution(8014491518241754523)
XLA Ops:
  0.6 107.0 %ffn.1 = (bf16[64,512]{1,0:T(8,128)(2,1)S(1)}, bf16[64,512]{1,0:T(8,128)(2,1)S(1)}, bf16[512,896]{1,0:T(8,128)(2,1)S(1)}, bf16[512,896]{1,0:T(8,128)(2,1)S(1)}, bf16[896,512]{1,0:T(8,128)(2,1)S(1)}) custom-call(bf16[64,512]{1,0:T(8,128)(2,1)} %tok_in.1, bf16[64,512]{1,0:T(8,128)(2,1)} %cot_in.1, bf16[512,896]{1,0:T(8,128)(2,1)} %wg_in.1, ...), custom_call_target="tpu_custom_call" | custom-call | tf_op jit(solution)/shard_map/ffn/pallas_call | solution.py:624
  107.6 1.6 %store.1 = (bf16[64,512]{1,0:T(8,128)(2,1)}, bf16[64,512]{1,0:T(8,128)(2,1)}, bf16[512,896]{1,0:T(8,128)(2,1)}, bf16[512,896]{1,0:T(8,128)(2,1)}, bf16[896,512]{1,0:T(8,128)(2,1)}) custom-call(bf16[64,512]{1,0:T(8,128)(2,1)S(1)} %get-tuple-element.10.refs_0_, bf16[64,512]{1,0:T(8,128)(2,1)S(1)} %get-tuple-element.11.refs_1_, ...), custom_call_target="tpu_custom_call" | custom-call | tf_op jit(solution)/shard_map/store/pallas_call | solution.py:663

commit v5 on v4

--- a/solution.py
+++ b/solution.py
@@ -199,17 +199,17 @@
     ("Z", 0, 0, 1, 1),
     ("W", 0, 0),
     ("Z", 1, 1, 0, 4),
+    ("Z", 1, 1, 1, 4),
     ("W", 0, 1),
     ("Z", 1, 0, 0, 1),
-    ("W", 1, 0),
-    ("Z", 1, 1, 1, 4),
-    ("Y", 0, 0, 0),
-    ("W", 1, 1),
     ("Z", 0, 1, 0, 3),
     ("Z", 0, 1, 1, 3),
+    ("W", 1, 0),
     ("Z", 1, 0, 1, 1),
+    ("Z", 1, 1, 0, 3),
+    ("W", 1, 1),
+    ("Y", 0, 0, 0),
     ("Y", 0, 0, 1),
-    ("Z", 1, 1, 0, 3),
     ("Y", 1, 0, 0),
     ("Z", 1, 1, 1, 3),
     ("Z", 0, 1, 0, 2),

time: 110 us -> 110 us (level)
  no operation moved by 1% of the time
where the time goes in v5:
time: 110 us; the launch traced here: 109 us
  Pallas kernels  108 us (98%)
    pallas_call x1, Pallas kernels, shards(): pl.pallas_call(kernel, out_shape=[pltpu.VMEM(shape, BF) for shape in shap...  106 us

profile of v5, /device:TPU:8, one launch (start us, length us, event | category | flops | bytes accessed | tf_op | source)
XLA Modules:
  0.0 108.7 jit_solution(8163162321540688206)
XLA Ops:
  0.6 106.4 %ffn.1 = (bf16[64,512]{1,0:T(8,128)(2,1)S(1)}, bf16[64,512]{1,0:T(8,128)(2,1)S(1)}, bf16[512,896]{1,0:T(8,128)(2,1)S(1)}, bf16[512,896]{1,0:T(8,128)(2,1)S(1)}, bf16[896,512]{1,0:T(8,128)(2,1)S(1)}) custom-call(bf16[64,512]{1,0:T(8,128)(2,1)} %tok_in.1, bf16[64,512]{1,0:T(8,128)(2,1)} %cot_in.1, bf16[512,896]{1,0:T(8,128)(2,1)} %wg_in.1, ...), custom_call_target="tpu_custom_call" | custom-call | tf_op jit(solution)/shard_map/ffn/pallas_call | solution.py:624
  107.1 1.6 %store.1 = (bf16[64,512]{1,0:T(8,128)(2,1)}, bf16[64,512]{1,0:T(8,128)(2,1)}, bf16[512,896]{1,0:T(8,128)(2,1)}, bf16[512,896]{1,0:T(8,128)(2,1)}, bf16[896,512]{1,0:T(8,128)(2,1)}) custom-call(bf16[64,512]{1,0:T(8,128)(2,1)S(1)} %get-tuple-element.10.refs_0_, bf16[64,512]{1,0:T(8,128)(2,1)S(1)} %get-tuple-element.11.refs_1_, ...), custom_call_target="tpu_custom_call" | custom-call | tf_op jit(solution)/shard_map/store/pallas_call | solution.py:663
